TPU v7x, 512 devices: a whole 4x8x8 slice. The times are simulated.
512 devices in a mesh: tm: 64 (over z_lo, y, core), band: 8 (over z_hi, x).
Axes of the slice: x: 4, y: 8, z: 8 (z_hi: 2, z_lo: 4; z = z_hi * 4 + z_lo), core: 2. Of those that a mesh axis runs over, the one named last changes fastest.
Arguments:
- feats: bfloat16 [64, 64, 128, 256], P('tm', 'band'), may hold values from -6 to 6
- cotangent: bfloat16 [64, 64, 128, 256], P('tm', 'band'), may hold values from -6 to 6
- w_value: bfloat16 [256, 256], replicated, may hold values from -0.375 to 0.375
- w_logit: bfloat16 [256, 48], replicated, may hold values from -24 to 24
- w_out: bfloat16 [256, 256], replicated, may hold values from -0.375 to 0.375
- row_offsets: int32 [64, 5, 64, 128], P('tm', None, 'band'), may hold values from -1 to 0
- col_offsets: int32 [64, 5, 64, 128], P('tm', None, 'band'), may hold values from -8 to 7
- fractions: int32 [64, 2, 5, 64, 128], P('tm', None, None, 'band'), may hold values from 0 to 7
- present: int32 [64, 5], P('tm'), may hold values 0 or 1
Outputs:
- grad_feats: bfloat16 [64, 64, 128, 256], P('tm', 'band')
- grad_w_value: float32 [256, 256], replicated
- grad_w_logit: float32 [256, 48], replicated
- grad_w_out: float32 [256, 256], replicated
All inputs are finite; a program needn't handle non-finite values. No bound on the sum of `present` on one device may be relied on, other than what follows from the above.
Results may differ from a plain program's by a relative error of at most 0.014.
Values may be sent and summed in bfloat16 or wider, within the bound.
No kernel may reach another device: no remote copies, remote signals or barrier semaphores. Data moves between devices by JAX's collectives and lax.ppermute only.
A program may use at most 64 MiB of HBM per device.

v0:
```python
import math

import jax
import numpy as np
import jax.numpy as jnp
from jax import lax
from jax.experimental import pallas as pl
from jax.experimental.pallas import tpu as pltpu
from jax.sharding import PartitionSpec as P


H = 8
E = 32
K = 5
J = 6
C = 256
COLS = 128
ROWS = 8
CELLS = ROWS * COLS
EXT = CELLS + 2 * COLS
PAY = 384
DISTANCES = (1, 2, 4, 8, 16)
SLOTS = (4, 1, 0, 2, 3)

TM = ("pair", "core")

F32 = jnp.float32
BF16 = jnp.bfloat16


def mm(a, b, ca, cb):
    return lax.dot_general(a, b, (((ca,), (cb,)), ((), ())), preferred_element_type=F32)


def iota(shape, dim):
    return lax.broadcasted_iota(jnp.int32, shape, dim)


def head_spread():
    return jnp.where(iota((H, C), 1) // E == iota((H, C), 0), 1.0, 0.0).astype(BF16)


def head_sums(spread, prod):
    high = prod.astype(BF16)
    low = (prod - high.astype(F32)).astype(BF16)
    return mm(spread, high, 1, 1) + mm(spread, low, 1, 1)


def rows_of(r):
    return pl.ds(r * COLS, COLS)


def prep_body(
    present, feats_hbm, cot_hbm, w_value_hbm, w_logit_hbm, w_out_hbm, row_hbm, col_hbm, fracs_hbm,
    values, attn, packets, dattn, accum, gwo, wl_t,
    mix, feats, cot, w_value, w_logit, w_out, row_off, col_off, fracs, sems,
):
    frame = lax.axis_index(TM)
    moves = (
        (w_logit_hbm, w_logit), (w_value_hbm, w_value), (feats_hbm, feats), (row_hbm, row_off),
        (col_hbm, col_off), (fracs_hbm, fracs), (w_out_hbm, w_out), (cot_hbm, cot),
    )
    copies = [pltpu.make_async_copy(src, dst, sems.at[i]) for i, (src, dst) in enumerate(moves)]
    for copy in copies:
        copy.start()
    for copy in copies:
        copy.wait()
    r48 = iota((H * J, H * J), 0)
    c48 = iota((H * J, H * J), 1)
    order = jnp.where(c48 == (r48 % H) * J + r48 // H, 1.0, 0.0).astype(BF16)
    wl = mm(order, w_logit[...], 1, 0).astype(BF16)
    wl_t[...] = wl
    spread = head_spread()
    valid = [None]
    for k in range(K):
        valid.append((present[0, k] == 1) & (frame >= DISTANCES[k]))
    accum[pl.ds(0, COLS), :] = jnp.zeros((COLS, C), F32)
    accum[pl.ds(EXT - COLS, COLS), :] = jnp.zeros((COLS, C), F32)
    for r in range(ROWS):
        f = feats[rows_of(r), :]
        v = mm(f, w_value[...], 1, 0).astype(BF16)
        values[rows_of(r), :] = v
        logits = mm(wl, f, 1, 1)
        masked = [logits[0:H]]
        for k in range(K):
            part = logits[(k + 1) * H : (k + 2) * H]
            masked.append(jnp.where(valid[k + 1], part, -1e30))
        top = masked[0]
        for part in masked[1:]:
            top = jnp.maximum(top, part)
        expo = [jnp.exp(masked[0] - top)]
        for k in range(K):
            expo.append(jnp.where(valid[k + 1], jnp.exp(masked[k + 1] - top), 0.0))
        total = expo[0]
        for part in expo[1:]:
            total = total + part
        weights = [part / total for part in expo]
        attn[:, rows_of(r)] = jnp.concatenate(weights, axis=0)
        for k in range(K):
            head = jnp.concatenate(
                [
                    weights[k + 1],
                    col_off[k, r : r + 1, :].astype(F32),
                    row_off[k, r : r + 1, :].astype(F32),
                    fracs[0, k, r : r + 1, :].astype(F32),
                    fracs[1, k, r : r + 1, :].astype(F32),
                    jnp.zeros((4, COLS), F32),
                ],
                axis=0,
            )
            packets[k, :, rows_of(r)] = head.astype(BF16)
        wide = mm(weights[0].astype(BF16), spread, 0, 0)
        dm = mm(cot[rows_of(r), :], w_out[...], 1, 1).astype(BF16).astype(F32)
        vf = v.astype(F32)
        dattn[:, rows_of(r)] = head_sums(spread, dm * vf)
        accum[rows_of(r + 1), :] = (wide * dm).astype(BF16).astype(F32)
        mix[rows_of(r), :] = (wide * vf).astype(BF16)
    gwo[...] = mm(mix[...], cot[...], 0, 0)


def slot_body(cot, packet, ext, w_out, accum_in, gwo_in, dattn, accum, gwo, mix):
    spread = head_spread()
    src = iota((COLS, COLS), 0).astype(F32)
    lane = iota((1, COLS), 1).astype(F32)
    accum[...] = accum_in[...]
    for r in range(ROWS):
        pack = packet[:, rows_of(r)]
        info = pack[8:16].astype(F32)
        c0 = lane + info[0:1]
        up = info[1:2] < -0.5
        a = info[2:3] * (1.0 / 64.0)
        b = info[3:4]
        near = 0.125 - a
        columns = jnp.where(src == c0, 8.0 - b, 0.0) + jnp.where(src == c0 + 1.0, b, 0.0)
        w0 = jnp.where(up, near, 0.0)
        w1 = jnp.where(up, a, near)
        w2 = jnp.where(up, 0.0, a)
        table = jnp.concatenate(
            [(columns * w0).astype(BF16), (columns * w1).astype(BF16), (columns * w2).astype(BF16)],
            axis=0,
        )
        window = pl.ds(r * COLS, 3 * COLS)
        taken = mm(table, ext[window, :], 0, 0).astype(BF16).astype(F32)
        wide = mm(pack[0:H], spread, 0, 0)
        dm = mm(cot[rows_of(r), :], w_out[...], 1, 1).astype(BF16).astype(F32)
        dattn[:, rows_of(r)] = head_sums(spread, dm * taken)
        mix[rows_of(r), :] = (wide * taken).astype(BF16)
        accum[window, :] += mm(table, (wide * dm).astype(BF16), 1, 0)
    gwo[...] = gwo_in[...] + mm(mix[...], cot[...], 0, 0)


def final_body(
    feats, cot, w_value, wl_t, attn, d0, d1, d2, d3, d4, d5, accum, from_prev, from_next, gwo,
    grad_feats, keep, send, dv, dl_a, dl_b,
):
    grads = (d0, d1, d2, d3, d4, d5)
    r48 = iota((H * J, COLS), 0)
    c48 = iota((H * J, COLS), 1)
    column = (r48 % H) * J + r48 // H
    half = H * J // 2
    first = jnp.where((c48 < half) & (column == c48), 1.0, 0.0).astype(BF16)
    second = jnp.where((c48 < half) & (column == c48 + half), 1.0, 0.0).astype(BF16)
    for r in range(ROWS):
        center = accum[rows_of(r + 1), :]
        if r == 0:
            center = center + from_prev[...].astype(F32)
        if r == ROWS - 1:
            center = center + from_next[...].astype(F32)
        low = center.astype(BF16)
        dv[rows_of(r), :] = low
        weights = [attn[pl.ds(j * H, H), rows_of(r)] for j in range(J)]
        terms = [grads[j][:, rows_of(r)] for j in range(J)]
        mean = weights[0] * terms[0]
        for j in range(1, J):
            mean = mean + weights[j] * terms[j]
        dl = jnp.concatenate(
            [weights[j] * (terms[j] - mean) for j in range(J)], axis=0
        ).astype(BF16)
        dl_a[rows_of(r), :] = mm(dl, first, 0, 0).astype(BF16)
        dl_b[rows_of(r), :] = mm(dl, second, 0, 0).astype(BF16)
        out = cot[rows_of(r), :].astype(F32) + mm(low, w_value[...], 1, 1)
        out = out + mm(dl, wl_t[...], 0, 0)
        grad_feats[rows_of(r), :] = out.astype(BF16)
    core = lax.axis_index("core")
    for mine in (0, 1):

        @pl.when(core == mine)
        def _():
            upper, lower = (keep, send) if mine == 0 else (send, keep)
            upper[:, pl.ds(0, C)] = gwo[...]
            upper[:, pl.ds(C, COLS)] = mm(feats[...], dl_a[...], 0, 0)
            lower[:, pl.ds(0, C)] = mm(feats[...], dv[...], 0, 0)
            lower[:, pl.ds(C, COLS)] = mm(feats[...], dl_b[...], 0, 0)


VM = pl.BlockSpec(memory_space=pltpu.VMEM)
SM = pl.BlockSpec(memory_space=pltpu.SMEM)
HB = pl.BlockSpec(memory_space=pltpu.HBM)


def sds(shape, dtype):
    return jax.ShapeDtypeStruct(shape, dtype)


def cost(flops, nbytes):
    return pl.CostEstimate(flops=flops, bytes_accessed=nbytes, transcendentals=0)


PARAMS = pltpu.CompilerParams(vmem_limit_bytes=48 * 1024 * 1024)


def prep(present, feats, cot, w_value, w_logit, w_out, row_off, col_off, fracs):
    return pl.pallas_call(
        prep_body,
        name="prep",
        out_shape=(
            sds((CELLS, C), BF16),
            sds((H * J, CELLS), F32),
            sds((K, 16, CELLS), BF16),
            sds((H, CELLS), F32),
            sds((EXT, C), F32),
            sds((C, C), F32),
            sds((H * J, C), BF16),
        ),
        in_specs=[SM] + [HB] * 8,
        out_specs=(VM,) * 7,
        scratch_shapes=[
            pltpu.VMEM((CELLS, C), BF16),
            pltpu.VMEM((CELLS, C), BF16),
            pltpu.VMEM((CELLS, C), BF16),
            pltpu.VMEM((C, C), BF16),
            pltpu.VMEM((H * J, C), BF16),
            pltpu.VMEM((C, C), BF16),
            pltpu.VMEM((K, ROWS, COLS), jnp.int32),
            pltpu.VMEM((K, ROWS, COLS), jnp.int32),
            pltpu.VMEM((2, K, ROWS, COLS), jnp.int32),
            pltpu.SemaphoreType.DMA((8,)),
        ],
        compiler_params=PARAMS,
        cost_estimate=cost(10**9, 4 * 10**6),
    )(
        present,
        *(
            pltpu.with_memory_space_constraint(x, pltpu.HBM)
            for x in (feats, cot, w_value, w_logit, w_out, row_off, col_off, fracs)
        ),
    )


def slot_call(cot, packet, ext, w_out, accum, gwo):
    return pl.pallas_call(
        slot_body,
        name="slot",
        out_shape=(sds((H, CELLS), F32), sds((EXT, C), F32), sds((C, C), F32)),
        in_specs=[VM] * 6,
        out_specs=(VM,) * 3,
        scratch_shapes=[pltpu.VMEM((CELLS, C), BF16)],
        input_output_aliases={4: 1, 5: 2},
        compiler_params=PARAMS,
        cost_estimate=cost(10**9, 4 * 10**6),
    )(cot, packet, ext, w_out, accum, gwo)


def final(*args):
    return pl.pallas_call(
        final_body,
        name="final",
        out_shape=(sds((CELLS, C), BF16), sds((C, PAY), F32), sds((C, PAY), F32)),
        in_specs=[VM] * 15,
        out_specs=(VM,) * 3,
        scratch_shapes=[
            pltpu.VMEM((CELLS, C), BF16),
            pltpu.VMEM((CELLS, COLS), BF16),
            pltpu.VMEM((CELLS, COLS), BF16),
        ],
        compiler_params=PARAMS,
        cost_estimate=cost(10**9, 4 * 10**6),
    )(*args)


def size(axis):
    return math.prod(lax.axis_size(a) for a in axis) if isinstance(axis, tuple) else lax.axis_size(axis)


def shifted(value, axis, steps):
    count = size(axis)
    initial, last = (max(0, -steps), min(count, count - steps))
    return lax.ppermute(value, axis, [(source, source + steps) for source in range(initial, last)])


def layer(feats, cotangent, w_value, w_logit, w_out, row_offsets, col_offsets, fractions, present):
    inputs = feats.reshape(CELLS, C)
    grad_out = cotangent.reshape(CELLS, C)
    count = size(TM)
    cots = [None] * K
    cots[1] = shifted(grad_out, TM, -2)
    cots[4] = shifted(grad_out, TM, -16)
    near = lax.ppermute(grad_out, TM, [(i, i - 1) for i in range(1, count, 2)])
    cots[3] = shifted(grad_out, TM, -8)
    values, attn, packets, d0, accum, gwo, wl_t = prep(
        present, inputs, grad_out, w_value, w_logit.T, w_out, row_offsets[0], col_offsets[0], fractions[0]
    )
    cots[2] = shifted(cots[1], TM, -2)
    far = lax.ppermute(cots[1], TM, [(i, i + 1) for i in range(0, count, 2)])
    cots[0] = near + far
    packs = [None] * K
    for k in SLOTS:
        packs[k] = shifted(packets[k], TM, -DISTANCES[k])
    low = shifted(values[CELLS - COLS :], "band", 1)
    high = shifted(values[:COLS], "band", -1)
    ext = jnp.concatenate([low, values, high], axis=0)
    grads = [None] * K
    back = [None] * K
    for k in SLOTS:
        grads[k], accum, gwo = slot_call(cots[k], packs[k], ext, w_out, accum, gwo)
        back[k] = shifted(grads[k], TM, DISTANCES[k])
    from_next = shifted(accum[:COLS].astype(BF16), "band", -1)
    from_prev = shifted(accum[EXT - COLS :].astype(BF16), "band", 1)
    grad_feats, keep, send = final(
        inputs, grad_out, w_value, wl_t, attn, d0, *back, accum, from_prev, from_next, gwo
    )
    swap = [(0, 1), (1, 0)]
    both = ("pair", "band")
    count = size(both)
    share = C // count
    part = keep + lax.ppermute(send, "core", swap)
    pieces = lax.all_to_all(part, both, 0, 0, tiled=True)
    mine = jnp.sum(pieces.reshape(count, share, PAY), axis=0)
    spread = jnp.broadcast_to(mine[None], (count, share, PAY)).reshape(C, PAY)
    own = lax.all_to_all(spread, both, 0, 0, tiled=True)
    other = lax.ppermute(own, "core", swap)
    first = lax.axis_index("core") == 0
    upper = jnp.where(first, own, other)
    lower = jnp.where(first, other, own)
    half = H * J // 2
    gwl = jnp.concatenate([upper[:, C : C + half], lower[:, C : C + half]], axis=1)
    return (grad_feats.reshape(feats.shape), lower[:, :C], gwl, upper[:, :C])


def solution(mesh):
    frames, bands = mesh.shape["tm"], mesh.shape["band"]
    inner = jax.sharding.Mesh(
        np.asarray(mesh.devices).reshape(frames // 2, 2, bands), ("pair", "core", "band")
    )
    placed = (
        P(TM, "band", None, None),
        P(TM, "band", None, None),
        P(),
        P(),
        P(),
        P(TM, None, "band", None),
        P(TM, None, "band", None),
        P(TM, None, None, "band", None),
        P(TM, None),
    )
    return jax.shard_map(
        layer,
        mesh=inner,
        in_specs=placed,
        out_specs=(P(TM, "band", None, None), P(), P(), P()),
        check_vma=False,
    )
```

profile of v0, /device:TPU:1, one launch (start us, length us, event | category | flops | bytes accessed | tf_op | source)
XLA Modules:
  0.0 206.6 jit_solution(1421024930953581575)
XLA Ops:
  0.6 1.3 collective-permute-start.7
  1.9 1.3 collective-permute-start.1
  3.9 5.3 %prep.1 = (bf16[1024,256]{1,0:T(8,128)(2,1)S(1)}, f32[48,1024]{1,0:T(8,128)S(1)}, bf16[5,16,1024]{2,1,0:T(8,128)(2,1)S(1)}, f32[8,1024]{1,0:T(8,128)S(1)}, f32[1...) custom-call(s32[1,5]{1,0:T(1,128)S(1)} %copy-done.4, bf16[1024,256]{1,0:T(8,128)(2,1)} %bitcast.26, ...), custom_call_target="tpu_custom_call" | custom-call | flops 1000000000 | bytes 4000000 | tf_op jit(solution)/shard_map/prep/pallas_call | solution.py:213
  9.2 4.1 %collective-permute-start.4 = (bf16[128,256]{1,0:T(8,128)(2,1)S(1)}, bf16[128,256]{1,0:T(8,128)(2,1)S(1)}, u32[]{:S(2)}, u32[]{:S(2)}) collective-permute-start(bf16[128,256]{1,0:T(8,128)(2,1)S(1)} %get-tuple-element.63), channel_id=1, source_target_pairs={{0,1},{1,2},{2,3},{3,4},{4,5},{5,6},{6,7},{8,9},{9,10},{10,11},{11... | collective-permute-start | bytes 196616 | tf_op jit(solution)/shard_map/ppermute | solution.py:288
  13.3 1.3 collective-permute-start.8
  14.6 6.1 %collective-permute-start = (bf16[1024,256]{1,0:T(8,128)(2,1)S(1)}, bf16[1024,256]{1,0:T(8,128)(2,1)S(1)}, u32[]{:S(2)}, u32[]{:S(2)}) collective-permute-start(bf16[1024,256]{1,0:T(8,128)(2,1)S(1)} %bitcast.31), channel_id=1, source_target_pairs={{8,0},{24,16},{40,32},{56,48},{72,64},{88,80},{104,96},{120,112},{... | collective-permute-start | bytes 1572872 | tf_op jit(solution)/shard_map/ppermute | solution.py:298
  22.8 1.3 collective-permute-start.2
  24.1 1.3 collective-permute-start.11
  27.9 1.3 collective-permute-start.6
  29.2 3.1 %slot.5 = (f32[8,1024]{1,0:T(8,128)S(1)}, f32[1280,256]{1,0:T(8,128)S(1)}, f32[256,256]{1,0:T(8,128)S(1)}) custom-call(bf16[1024,256]{1,0:T(8,128)(2,1)S(1)} %collective-permute-done.7.cot, bf16[16,1024]{1,0:T(8,128)(2,1)S(1)} %collective-permute-done.8.packet, ...), custom_call_target="tpu_custom_call", output_to_operand_aliasing={{1}: (4, {}), {2}: (5, {})} | custom-call | flops 1000000000 | bytes 4000000 | tf_op jit(solution)/shard_map/slot/pallas_call | solution.py:251
  32.2 5.2 %collective-permute-done.6.packet = bf16[16,1024]{1,0:T(8,128)(2,1)S(1)} collective-permute-done((bf16[16,1024]{1,0:T(8,128)(2,1)S(1)}, bf16[16,1024]{1,0:T(8,128)(2,1)S(1)}, u32[]{:S(2)}, u32[]{:S(2)}) %collective-permute-start.6) | collective-permute-done | bytes 32800 | tf_op jit(solution)/shard_map/ppermute | solution.py:288
  37.5 5.7 %collective-permute-start.3 = (bf16[16,1024]{1,0:T(8,128)(2,1)S(1)}, bf16[16,1024]{1,0:T(8,128)(2,1)S(1)}, u32[]{:S(2)}, u32[]{:S(2)}) collective-permute-start(bf16[16,1024]{1,0:T(8,128)(2,1)S(1)} %get-tuple-element.68), channel_id=1, source_target_pairs={{8,0},{16,8},{24,16},{32,24},{40,32},{48,40},{56,48},{64,56},{72,6... | collective-permute-start | bytes 98312 | tf_op jit(solution)/shard_map/ppermute | solution.py:288
  43.1 3.0 %slot.6 = (f32[8,1024]{1,0:T(8,128)S(1)}, f32[1280,256]{1,0:T(8,128)S(1)}, f32[256,256]{1,0:T(8,128)S(1)}) custom-call(bf16[1024,256]{1,0:T(8,128)(2,1)S(1)} %collective-permute-done.1.cot, bf16[16,1024]{1,0:T(8,128)(2,1)S(1)} %collective-permute-done.6.packet, ...), custom_call_target="tpu_custom_call", output_to_operand_aliasing={{1}: (4, {}), {2}: (5, {})} | custom-call | flops 1000000000 | bytes 4000000 | tf_op jit(solution)/shard_map/slot/pallas_call | solution.py:251
  46.2 1.3 collective-permute-start.12
  47.5 1.3 collective-permute-start.15
  49.0 4.2 %collective-permute-start.10 = (f32[8,1024]{1,0:T(8,128)S(1)}, f32[8,1024]{1,0:T(8,128)S(1)}, u32[]{:S(2)}, u32[]{:S(2)}) collective-permute-start(f32[8,1024]{1,0:T(8,128)S(1)} %get-tuple-element.41), channel_id=1, source_target_pairs={{0,16},{8,24},{16,32},{24,40},{32,48},{40,56},{48,64},{56,72},{64,... | collective-permute-start | bytes 98312 | tf_op jit(solution)/shard_map/ppermute | solution.py:288
  53.2 3.0 %slot.7 = (f32[8,1024]{1,0:T(8,128)S(1)}, f32[1280,256]{1,0:T(8,128)S(1)}, f32[256,256]{1,0:T(8,128)S(1)}) custom-call(bf16[1024,256]{1,0:T(8,128)(2,1)S(1)} %add.6.cot, bf16[16,1024]{1,0:T(8,128)(2,1)S(1)} %collective-permute-done.3.packet, ...), custom_call_target="tpu_custom_call", output_to_operand_aliasing={{1}: (4, {}), {2}: (5, {})} | custom-call | flops 1000000000 | bytes 4000000 | tf_op jit(solution)/shard_map/slot/pallas_call | solution.py:251
  56.3 38.7 %collective-permute-start.17 = (f32[8,1024]{1,0:T(8,128)S(1)}, f32[8,1024]{1,0:T(8,128)S(1)}, u32[]{:S(2)}, u32[]{:S(2)}) collective-permute-start(f32[8,1024]{1,0:T(8,128)S(1)} %get-tuple-element.48), channel_id=1, source_target_pairs={{0,128},{8,136},{16,144},{24,152},{32,160},{40,168},{48,176},{56,1... | collective-permute-start | bytes 98312 | tf_op jit(solution)/shard_map/ppermute | solution.py:288
  95.0 3.1 %slot.8 = (f32[8,1024]{1,0:T(8,128)S(1)}, f32[1280,256]{1,0:T(8,128)S(1)}, f32[256,256]{1,0:T(8,128)S(1)}) custom-call(bf16[1024,256]{1,0:T(8,128)(2,1)S(1)} %collective-permute-done.11.cot, bf16[16,1024]{1,0:T(8,128)(2,1)S(1)} %collective-permute-done.12.packet, ...), custom_call_target="tpu_custom_call", output_to_operand_aliasing={{1}: (4, {}), {2}: (5, {})} | custom-call | flops 1000000000 | bytes 4000000 | tf_op jit(solution)/shard_map/slot/pallas_call | solution.py:251
  98.1 3.1 %slot.9 = (f32[8,1024]{1,0:T(8,128)S(1)}, f32[1280,256]{1,0:T(8,128)S(1)}, f32[256,256]{1,0:T(8,128)S(1)}) custom-call(bf16[1024,256]{1,0:T(8,128)(2,1)S(1)} %collective-permute-done.14.cot, bf16[16,1024]{1,0:T(8,128)(2,1)S(1)} %collective-permute-done.15.packet, ...), custom_call_target="tpu_custom_call", output_to_operand_aliasing={{1}: (4, {}), {2}: (5, {})} | custom-call | flops 1000000000 | bytes 4000000 | tf_op jit(solution)/shard_map/slot/pallas_call | solution.py:251
  101.2 4.1 %collective-permute-start.18 = (bf16[128,256]{1,0:T(8,128)(2,1)S(1)}, bf16[128,256]{1,0:T(8,128)(2,1)S(1)}, u32[]{:S(2)}, u32[]{:S(2)}) collective-permute-start(bf16[128,256]{1,0:T(8,128)(2,1)S(1)} %get-tuple-element.61), channel_id=1, source_target_pairs={{0,1},{1,2},{2,3},{3,4},{4,5},{5,6},{6,7},{8,9},{9,10},{10,11},{11... | collective-permute-start | bytes 196616 | tf_op jit(solution)/shard_map/ppermute | solution.py:288
  105.4 1.3 collective-permute-start.19
  106.7 7.3 %collective-permute-start.16 = (f32[8,1024]{1,0:T(8,128)S(1)}, f32[8,1024]{1,0:T(8,128)S(1)}, u32[]{:S(2)}, u32[]{:S(2)}) collective-permute-start(f32[8,1024]{1,0:T(8,128)S(1)} %get-tuple-element.47), channel_id=1, source_target_pairs={{0,64},{8,72},{16,80},{24,88},{32,96},{40,104},{48,112},{56,120},{... | collective-permute-start | bytes 98312 | tf_op jit(solution)/shard_map/ppermute | solution.py:288
  113.9 1.3 collective-permute-start.13
  115.3 3.6 %collective-permute-start.9 = (f32[8,1024]{1,0:T(8,128)S(1)}, f32[8,1024]{1,0:T(8,128)S(1)}, u32[]{:S(2)}, u32[]{:S(2)}) collective-permute-start(f32[8,1024]{1,0:T(8,128)S(1)} %get-tuple-element.40), channel_id=1, source_target_pairs={{0,8},{8,16},{16,24},{24,32},{32,40},{40,48},{48,56},{56,64},{64,7... | collective-permute-start | bytes 98312 | tf_op jit(solution)/shard_map/ppermute | solution.py:288
  119.9 2.3 %final.1 = (bf16[1024,256]{1,0:T(8,128)(2,1)}, f32[256,384]{1,0:T(8,128)S(1)}, f32[256,384]{1,0:T(8,128)S(1)}) custom-call(bf16[1024,256]{1,0:T(8,128)(2,1)S(1)} %bitcast.27, bf16[1024,256]{1,0:T(8,128)(2,1)S(1)} %bitcast.33, bf16[256,256]{1,0:T(8,128)(2,1)S(1)} %copy-done.3, bf16[48,256]{1,0:T(8,128)(2,1)S(1)} %get-tuple-element.29.wl_t, ...), custom_call_target="tpu_custom_call" | custom-call | flops 1000000000 | bytes 4000000 | tf_op jit(solution)/shard_map/final/pallas_call | solution.py:265
  122.2 1.9 collective-permute-start.20
  124.1 1.7 collective-permute-done.20
  126.3 45.9 %all_to_all.18 = f32[256,1,384]{2,1,0:T(1,128)S(1)} all-to-all(f32[256,1,384]{2,1,0:T(1,128)S(1)} %copy.24), channel_id=1, replica_groups=mesh['pair'=32,'core'=2,'band'=8] {'pair','band'}, dimensions={0} | all-to-all | bytes 786432 | tf_op jit(solution)/shard_map/all_to_all | solution.py:327
  172.7 25.5 %all_to_all.19 = f32[256,1,384]{2,1,0:T(1,128)S(1)} all-to-all(f32[256,1,384]{2,1,0:T(1,128)S(1)} %reshape.36), channel_id=1, replica_groups=mesh['pair'=32,'core'=2,'band'=8] {'pair','band'}, dimensions={0} | all-to-all | bytes 786432 | tf_op jit(solution)/shard_map/all_to_all | solution.py:330
  198.2 4.7 %collective-permute-start.21 = (f32[256,384]{1,0:T(8,128)S(1)}, f32[256,384]{1,0:T(8,128)S(1)}, u32[]{:S(2)}, u32[]{:S(2)}) collective-permute-start(f32[256,384]{1,0:T(8,128)S(1)} %bitcast.34), channel_id=1, source_target_pairs={{0,8},{8,0},{1,9},{9,1},{2,10},{10,2},{3,11},{11,3},{4,12},{12,4},... | collective-permute-start | bytes 1179656 | tf_op jit(solution)/shard_map/ppermute | solution.py:331
  202.9 1.3 collective-permute-done.21
  (52 shorter events, 9.7 us)
Async XLA Ops:
  0.6 27.2 %collective-permute-start.7 = (bf16[1024,256]{1,0:T(8,128)(2,1)}, bf16[1024,256]{1,0:T(8,128)(2,1)S(1)}, u32[]{:S(2)}, u32[]{:S(2)}) collective-permute-start(bf16[1024,256]{1,0:T(8,128)(2,1)} %bitcast.28), channel_id=1, source_target_pairs={{128,0},{136,8},{144,16},{152,24},{160,32},{168,40},{176,48},{184,... | collective-permute-start | bytes 1572872 | tf_op jit(solution)/shard_map/ppermute | solution.py:288
  1.9 20.9 %collective-permute-start.1 = (bf16[1024,256]{1,0:T(8,128)(2,1)}, bf16[1024,256]{1,0:T(8,128)(2,1)S(1)}, u32[]{:S(2)}, u32[]{:S(2)}) collective-permute-start(bf16[1024,256]{1,0:T(8,128)(2,1)} %bitcast.29), channel_id=1, source_target_pairs={{16,0},{24,8},{32,16},{40,24},{48,32},{56,40},{64,48},{72,56},{80,... | collective-permute-start | bytes 1572872 | tf_op jit(solution)/shard_map/ppermute | solution.py:288
  3.2 0.7 copy-start.4
  3.9 10.7 %copy-start.1 = (bf16[1,8,128,256]{3,2,1,0:T(8,128)(2,1)S(1)}, bf16[1,8,128,256]{3,2,1,0:T(8,128)(2,1)}, u32[]{:S(2)}) copy-start(bf16[1,8,128,256]{3,2,1,0:T(8,128)(2,1)} %param.10) | copy-start | bytes 1572868
  9.2 20.0 %copy-start.2 = (bf16[256,256]{1,0:T(8,128)(2,1)S(1)}, bf16[256,256]{1,0:T(8,128)(2,1)}, u32[]{:S(2)}) copy-start(bf16[256,256]{1,0:T(8,128)(2,1)} %w_out.9) | copy-start | bytes 393220
  9.2 14.9 %collective-permute-start.4 = (bf16[128,256]{1,0:T(8,128)(2,1)S(1)}, bf16[128,256]{1,0:T(8,128)(2,1)S(1)}, u32[]{:S(2)}, u32[]{:S(2)}) collective-permute-start(bf16[128,256]{1,0:T(8,128)(2,1)S(1)} %get-tuple-element.63), channel_id=1, source_target_pairs={{0,1},{1,2},{2,3},{3,4},{4,5},{5,6},{6,7},{8,9},{9,10},{10,11},{11... | collective-permute-start | bytes 196616 | tf_op jit(solution)/shard_map/ppermute | solution.py:288
  13.3 8.2 %collective-permute-start.8 = (bf16[16,1024]{1,0:T(8,128)(2,1)S(1)}, bf16[16,1024]{1,0:T(8,128)(2,1)S(1)}, u32[]{:S(2)}, u32[]{:S(2)}) collective-permute-start(bf16[16,1024]{1,0:T(8,128)(2,1)S(1)} %get-tuple-element.66), channel_id=1, source_target_pairs={{128,0},{136,8},{144,16},{152,24},{160,32},{168,40},{176,48},{184,... | collective-permute-start | bytes 98312 | tf_op jit(solution)/shard_map/ppermute | solution.py:288
  14.6 31.6 %collective-permute-start = (bf16[1024,256]{1,0:T(8,128)(2,1)S(1)}, bf16[1024,256]{1,0:T(8,128)(2,1)S(1)}, u32[]{:S(2)}, u32[]{:S(2)}) collective-permute-start(bf16[1024,256]{1,0:T(8,128)(2,1)S(1)} %bitcast.31), channel_id=1, source_target_pairs={{8,0},{24,16},{40,32},{56,48},{72,64},{88,80},{104,96},{120,112},{... | collective-permute-start | bytes 1572872 | tf_op jit(solution)/shard_map/ppermute | solution.py:298
  21.5 5.0 %collective-permute-start.5 = (bf16[128,256]{1,0:T(8,128)(2,1)S(1)}, bf16[128,256]{1,0:T(8,128)(2,1)S(1)}, u32[]{:S(2)}, u32[]{:S(2)}) collective-permute-start(bf16[128,256]{1,0:T(8,128)(2,1)S(1)} %get-tuple-element.62), channel_id=1, source_target_pairs={{1,0},{2,1},{3,2},{4,3},{5,4},{6,5},{7,6},{9,8},{10,9},{11,10},{12... | collective-permute-start | bytes 196616 | tf_op jit(solution)/shard_map/ppermute | solution.py:288
  22.8 24.7 %collective-permute-start.2 = (bf16[1024,256]{1,0:T(8,128)(2,1)S(1)}, bf16[1024,256]{1,0:T(8,128)(2,1)S(1)}, u32[]{:S(2)}, u32[]{:S(2)}) collective-permute-start(bf16[1024,256]{1,0:T(8,128)(2,1)S(1)} %collective-permute-done.1.cot), channel_id=1, source_target_pairs={{0,8},{16,24},{32,40},{48,56},{64,72},{80,88},{96,104},{112,120},{... | collective-permute-start | bytes 1572872 | tf_op jit(solution)/shard_map/ppermute | solution.py:304
  24.1 70.8 %collective-permute-start.11 = (bf16[1024,256]{1,0:T(8,128)(2,1)S(1)}, bf16[1024,256]{1,0:T(8,128)(2,1)S(1)}, u32[]{:S(2)}, u32[]{:S(2)}) collective-permute-start(bf16[1024,256]{1,0:T(8,128)(2,1)S(1)} %collective-permute-done.1.cot), channel_id=1, source_target_pairs={{16,0},{24,8},{32,16},{40,24},{48,32},{56,40},{64,48},{72,56},{80,... | collective-permute-start | bytes 1572872 | tf_op jit(solution)/shard_map/ppermute | solution.py:288
  26.5 71.5 %collective-permute-start.14 = (bf16[1024,256]{1,0:T(8,128)(2,1)S(1)}, bf16[1024,256]{1,0:T(8,128)(2,1)S(1)}, u32[]{:S(2)}, u32[]{:S(2)}) collective-permute-start(bf16[1024,256]{1,0:T(8,128)(2,1)S(1)} %bitcast.32), channel_id=1, source_target_pairs={{64,0},{72,8},{80,16},{88,24},{96,32},{104,40},{112,48},{120,56},{... | collective-permute-start | bytes 1572872 | tf_op jit(solution)/shard_map/ppermute | solution.py:288
  27.9 9.6 %collective-permute-start.6 = (bf16[16,1024]{1,0:T(8,128)(2,1)S(1)}, bf16[16,1024]{1,0:T(8,128)(2,1)S(1)}, u32[]{:S(2)}, u32[]{:S(2)}) collective-permute-start(bf16[16,1024]{1,0:T(8,128)(2,1)S(1)} %get-tuple-element.67), channel_id=1, source_target_pairs={{16,0},{24,8},{32,16},{40,24},{48,32},{56,40},{64,48},{72,56},{80,... | collective-permute-start | bytes 98312 | tf_op jit(solution)/shard_map/ppermute | solution.py:288
  37.5 11.5 %collective-permute-start.3 = (bf16[16,1024]{1,0:T(8,128)(2,1)S(1)}, bf16[16,1024]{1,0:T(8,128)(2,1)S(1)}, u32[]{:S(2)}, u32[]{:S(2)}) collective-permute-start(bf16[16,1024]{1,0:T(8,128)(2,1)S(1)} %get-tuple-element.68), channel_id=1, source_target_pairs={{8,0},{16,8},{24,16},{32,24},{40,32},{48,40},{56,48},{64,56},{72,6... | collective-permute-start | bytes 98312 | tf_op jit(solution)/shard_map/ppermute | solution.py:288
  46.2 10.1 %collective-permute-start.12 = (bf16[16,1024]{1,0:T(8,128)(2,1)S(1)}, bf16[16,1024]{1,0:T(8,128)(2,1)S(1)}, u32[]{:S(2)}, u32[]{:S(2)}) collective-permute-start(bf16[16,1024]{1,0:T(8,128)(2,1)S(1)} %get-tuple-element.65), channel_id=1, source_target_pairs={{32,0},{40,8},{48,16},{56,24},{64,32},{72,40},{80,48},{88,56},{96,... | collective-permute-start | bytes 98312 | tf_op jit(solution)/shard_map/ppermute | solution.py:288
  47.5 50.5 %collective-permute-start.15 = (bf16[16,1024]{1,0:T(8,128)(2,1)S(1)}, bf16[16,1024]{1,0:T(8,128)(2,1)S(1)}, u32[]{:S(2)}, u32[]{:S(2)}) collective-permute-start(bf16[16,1024]{1,0:T(8,128)(2,1)S(1)} %get-tuple-element.64), channel_id=1, source_target_pairs={{64,0},{72,8},{80,16},{88,24},{96,32},{104,40},{112,48},{120,56},{... | collective-permute-start | bytes 98312 | tf_op jit(solution)/shard_map/ppermute | solution.py:288
  49.0 65.0 %collective-permute-start.10 = (f32[8,1024]{1,0:T(8,128)S(1)}, f32[8,1024]{1,0:T(8,128)S(1)}, u32[]{:S(2)}, u32[]{:S(2)}) collective-permute-start(f32[8,1024]{1,0:T(8,128)S(1)} %get-tuple-element.41), channel_id=1, source_target_pairs={{0,16},{8,24},{16,32},{24,40},{32,48},{40,56},{48,64},{56,72},{64,... | collective-permute-start | bytes 98312 | tf_op jit(solution)/shard_map/ppermute | solution.py:288
  56.3 59.0 %collective-permute-start.17 = (f32[8,1024]{1,0:T(8,128)S(1)}, f32[8,1024]{1,0:T(8,128)S(1)}, u32[]{:S(2)}, u32[]{:S(2)}) collective-permute-start(f32[8,1024]{1,0:T(8,128)S(1)} %get-tuple-element.48), channel_id=1, source_target_pairs={{0,128},{8,136},{16,144},{24,152},{32,160},{40,168},{48,176},{56,1... | collective-permute-start | bytes 98312 | tf_op jit(solution)/shard_map/ppermute | solution.py:288
  101.1 18.8 %copy-start = (bf16[1,8,128,256]{3,2,1,0:T(8,128)(2,1)S(1)}, bf16[1,8,128,256]{3,2,1,0:T(8,128)(2,1)}, u32[]{:S(2)}) copy-start(bf16[1,8,128,256]{3,2,1,0:T(8,128)(2,1)} %param.9) | copy-start | bytes 1572868
  101.1 18.8 %copy-start.3 = (bf16[256,256]{1,0:T(8,128)(2,1)S(1)}, bf16[256,256]{1,0:T(8,128)(2,1)}, u32[]{:S(2)}) copy-start(bf16[256,256]{1,0:T(8,128)(2,1)} %w_value.1) | copy-start | bytes 393220
  101.2 18.7 %collective-permute-start.18 = (bf16[128,256]{1,0:T(8,128)(2,1)S(1)}, bf16[128,256]{1,0:T(8,128)(2,1)S(1)}, u32[]{:S(2)}, u32[]{:S(2)}) collective-permute-start(bf16[128,256]{1,0:T(8,128)(2,1)S(1)} %get-tuple-element.61), channel_id=1, source_target_pairs={{0,1},{1,2},{2,3},{3,4},{4,5},{5,6},{6,7},{8,9},{9,10},{10,11},{11... | collective-permute-start | bytes 196616 | tf_op jit(solution)/shard_map/ppermute | solution.py:288
  105.4 14.6 %collective-permute-start.19 = (bf16[128,256]{1,0:T(8,128)(2,1)S(1)}, bf16[128,256]{1,0:T(8,128)(2,1)S(1)}, u32[]{:S(2)}, u32[]{:S(2)}) collective-permute-start(bf16[128,256]{1,0:T(8,128)(2,1)S(1)} %get-tuple-element.60), channel_id=1, source_target_pairs={{1,0},{2,1},{3,2},{4,3},{5,4},{6,5},{7,6},{9,8},{10,9},{11,10},{12... | collective-permute-start | bytes 196616 | tf_op jit(solution)/shard_map/ppermute | solution.py:288
  106.7 12.2 %collective-permute-start.16 = (f32[8,1024]{1,0:T(8,128)S(1)}, f32[8,1024]{1,0:T(8,128)S(1)}, u32[]{:S(2)}, u32[]{:S(2)}) collective-permute-start(f32[8,1024]{1,0:T(8,128)S(1)} %get-tuple-element.47), channel_id=1, source_target_pairs={{0,64},{8,72},{16,80},{24,88},{32,96},{40,104},{48,112},{56,120},{... | collective-permute-start | bytes 98312 | tf_op jit(solution)/shard_map/ppermute | solution.py:288
  113.9 5.0 %collective-permute-start.13 = (f32[8,1024]{1,0:T(8,128)S(1)}, f32[8,1024]{1,0:T(8,128)S(1)}, u32[]{:S(2)}, u32[]{:S(2)}) collective-permute-start(f32[8,1024]{1,0:T(8,128)S(1)} %get-tuple-element.44), channel_id=1, source_target_pairs={{0,32},{8,40},{16,48},{24,56},{32,64},{40,72},{48,80},{56,88},{64,... | collective-permute-start | bytes 98312 | tf_op jit(solution)/shard_map/ppermute | solution.py:288
  115.3 4.7 %collective-permute-start.9 = (f32[8,1024]{1,0:T(8,128)S(1)}, f32[8,1024]{1,0:T(8,128)S(1)}, u32[]{:S(2)}, u32[]{:S(2)}) collective-permute-start(f32[8,1024]{1,0:T(8,128)S(1)} %get-tuple-element.40), channel_id=1, source_target_pairs={{0,8},{8,16},{16,24},{24,32},{32,40},{40,48},{48,56},{56,64},{64,7... | collective-permute-start | bytes 98312 | tf_op jit(solution)/shard_map/ppermute | solution.py:288
  122.2 3.6 %collective-permute-start.20 = (f32[256,384]{1,0:T(8,128)S(1)}, f32[256,384]{1,0:T(8,128)S(1)}, u32[]{:S(2)}, u32[]{:S(2)}) collective-permute-start(f32[256,384]{1,0:T(8,128)S(1)} %get-tuple-element.53), channel_id=1, source_target_pairs={{0,8},{8,0},{1,9},{9,1},{2,10},{10,2},{3,11},{11,3},{4,12},{12,4},... | collective-permute-start | bytes 1179656 | tf_op jit(solution)/shard_map/ppermute | solution.py:326
  198.2 6.0 %collective-permute-start.21 = (f32[256,384]{1,0:T(8,128)S(1)}, f32[256,384]{1,0:T(8,128)S(1)}, u32[]{:S(2)}, u32[]{:S(2)}) collective-permute-start(f32[256,384]{1,0:T(8,128)S(1)} %bitcast.34), channel_id=1, source_target_pairs={{0,8},{8,0},{1,9},{9,1},{2,10},{10,2},{3,11},{11,3},{4,12},{12,4},... | collective-permute-start | bytes 1179656 | tf_op jit(solution)/shard_map/ppermute | solution.py:331
where the time goes:
time: 207 us
  starting transfers between devices  95.9 us (46%)
  blocking collectives  71.4 us (34%)
  Pallas kernels  22.8 us (11%)
  waiting for transfers between devices  11.1 us (5%)
  local copies, waits for them, and re-layouts  2.99 us (1%)
    ppermute x18, starting transfers between devices, shifted(): lax.ppermute(value, axis, [(source, source + steps) for source in range(i...  81.8 us
    all_to_all x1, blocking collectives, layer(): pieces = lax.all_to_all(part, both, 0, 0, tiled=True)  45.9 us
    all_to_all x1, blocking collectives, layer(): own = lax.all_to_all(spread, both, 0, 0, tiled=True)  25.5 us
    pallas_call x5, Pallas kernels, slot_call(): pl.pallas_call(slot_body, name='slot', out_shape=(sds((H, CELLS), F32), s...  15.3 us
    ppermute x18, waiting for transfers between devices, shifted(): lax.ppermute(value, axis, [(source, source + steps) for source in range(i...  8.08 us
    ppermute x1, starting transfers between devices, layer(): near = lax.ppermute(grad_out, TM, [(i, i - 1) for i in range(1, count, 2)])  6.13 us
    pallas_call x1, Pallas kernels, prep(): pl.pallas_call(prep_body, name='prep', out_shape=(sds((CELLS, C), BF16),...  5.29 us
    ppermute x1, starting transfers between devices, layer(): other = lax.ppermute(own, 'core', swap)  4.69 us
  transfers between devices with their start and end apart: 22, of which 6 were waited for; matrix products, arithmetic and copies ran while one was open for 0% of the time, Pallas kernels for 10%

commit v1 on v0

--- a/solution.py
+++ b/solution.py
@@ -1,3 +1,4 @@
+import functools
 import math
 
 import jax
@@ -19,6 +20,7 @@
 CELLS = ROWS * COLS
 EXT = CELLS + 2 * COLS
 PAY = 384
+PACK = 64
 DISTANCES = (1, 2, 4, 8, 16)
 SLOTS = (4, 1, 0, 2, 3)
 
@@ -52,7 +54,7 @@
 
 def prep_body(
     present, feats_hbm, cot_hbm, w_value_hbm, w_logit_hbm, w_out_hbm, row_hbm, col_hbm, fracs_hbm,
-    values, attn, packets, dattn, accum, gwo, wl_t,
+    values, attn, m16, m2, m1, m8, dattn, accum, gwo, wl_t,
     mix, feats, cot, w_value, w_logit, w_out, row_off, col_off, fracs, sems,
 ):
     frame = lax.axis_index(TM)
@@ -71,6 +73,15 @@
     wl = mm(order, w_logit[...], 1, 0).astype(BF16)
     wl_t[...] = wl
     spread = head_spread()
+    places = (
+        ((m1, CELLS), (m2, PACK + CELLS)),
+        ((m2, 2 * PACK + CELLS),),
+        ((m2, 0),),
+        ((m8, CELLS),),
+        ((m16, CELLS),),
+    )
+    for message, start in ((m16, 0), (m2, PACK), (m1, 0), (m8, 0)):
+        message[pl.ds(start, CELLS), :] = cot[...]
     valid = [None]
     for k in range(K):
         valid.append((present[0, k] == 1) & (frame >= DISTANCES[k]))
@@ -108,7 +119,9 @@
                 ],
                 axis=0,
             )
-            packets[k, :, rows_of(r)] = head.astype(BF16)
+            pack = head.astype(BF16)
+            for message, start in places[k]:
+                message[pl.ds(start + 16 * (r // 2), 16), pl.ds((r % 2) * COLS, COLS)] = pack
         wide = mm(weights[0].astype(BF16), spread, 0, 0)
         dm = mm(cot[rows_of(r), :], w_out[...], 1, 1).astype(BF16).astype(F32)
         vf = v.astype(F32)
@@ -118,13 +131,21 @@
     gwo[...] = mm(mix[...], cot[...], 0, 0)
 
 
-def slot_body(cot, packet, ext, w_out, accum_in, gwo_in, dattn, accum, gwo, mix):
+def ext_body(values, low, high, w_value, ext):
+    ext[pl.ds(0, COLS), :] = mm(low[...], w_value[...], 1, 0).astype(BF16)
+    ext[pl.ds(COLS, CELLS), :] = values[...]
+    ext[pl.ds(COLS + CELLS, COLS), :] = mm(high[...], w_value[...], 1, 0).astype(BF16)
+
+
+def slot_body(
+    cot_at, pack_at, message, ext, w_out, accum_in, gwo_in, dattn, accum, gwo, mix
+):
     spread = head_spread()
     src = iota((COLS, COLS), 0).astype(F32)
     lane = iota((1, COLS), 1).astype(F32)
     accum[...] = accum_in[...]
     for r in range(ROWS):
-        pack = packet[:, rows_of(r)]
+        pack = message[pl.ds(pack_at + 16 * (r // 2), 16), pl.ds((r % 2) * COLS, COLS)]
         info = pack[8:16].astype(F32)
         c0 = lane + info[0:1]
         up = info[1:2] < -0.5
@@ -142,55 +163,58 @@
         window = pl.ds(r * COLS, 3 * COLS)
         taken = mm(table, ext[window, :], 0, 0).astype(BF16).astype(F32)
         wide = mm(pack[0:H], spread, 0, 0)
-        dm = mm(cot[rows_of(r), :], w_out[...], 1, 1).astype(BF16).astype(F32)
+        cot = message[pl.ds(cot_at + r * COLS, COLS), :]
+        dm = mm(cot, w_out[...], 1, 1).astype(BF16).astype(F32)
         dattn[:, rows_of(r)] = head_sums(spread, dm * taken)
         mix[rows_of(r), :] = (wide * taken).astype(BF16)
         accum[window, :] += mm(table, (wide * dm).astype(BF16), 1, 0)
-    gwo[...] = gwo_in[...] + mm(mix[...], cot[...], 0, 0)
-
-
-def final_body(
-    feats, cot, w_value, wl_t, attn, d0, d1, d2, d3, d4, d5, accum, from_prev, from_next, gwo,
-    grad_feats, keep, send, dv, dl_a, dl_b,
-):
+    gwo[...] = gwo_in[...] + mm(mix[...], message[pl.ds(cot_at, CELLS), :], 0, 0)
+
+
+def value_body(feats, low, high, accum, gwo, keep, send, dv):
+    dv[...] = accum[...].astype(BF16)
+    gwv = mm(feats[...], dv[pl.ds(COLS, CELLS), :], 0, 0)
+    gwv = gwv + mm(low[...], dv[pl.ds(0, COLS), :], 0, 0)
+    gwv = gwv + mm(high[...], dv[pl.ds(COLS + CELLS, COLS), :], 0, 0)
+    core = lax.axis_index("core")
+    for mine in (0, 1):
+
+        @pl.when(core == mine)
+        def _():
+            keep[...] = gwo[...] if mine == 0 else gwv
+            send[...] = gwv if mine == 0 else gwo[...]
+
+
+def logit_body(feats, attn, d0, d1, d2, d3, d4, d5, keep, came, dl_t, pay, dl):
     grads = (d0, d1, d2, d3, d4, d5)
     r48 = iota((H * J, COLS), 0)
     c48 = iota((H * J, COLS), 1)
-    column = (r48 % H) * J + r48 // H
-    half = H * J // 2
-    first = jnp.where((c48 < half) & (column == c48), 1.0, 0.0).astype(BF16)
-    second = jnp.where((c48 < half) & (column == c48 + half), 1.0, 0.0).astype(BF16)
+    order = jnp.where(c48 == (r48 % H) * J + r48 // H, 1.0, 0.0).astype(BF16)
+    weights = [attn[pl.ds(j * H, H), :] for j in range(J)]
+    terms = [grads[j][...] for j in range(J)]
+    mean = weights[0] * terms[0]
+    for j in range(1, J):
+        mean = mean + weights[j] * terms[j]
+    low = jnp.concatenate(
+        [weights[j] * (terms[j] - mean) for j in range(J)], axis=0
+    ).astype(BF16)
+    dl_t[...] = low
+    for r in range(ROWS):
+        dl[rows_of(r), :] = mm(low[:, r * COLS : (r + 1) * COLS], order, 0, 0).astype(BF16)
+    pay[:, pl.ds(0, C)] = keep[...] + came[...]
+    pay[:, pl.ds(C, COLS)] = mm(feats[...], dl[...], 0, 0)
+
+
+def feats_body(cot, w_value, wl_t, dl_t, accum, from_prev, from_next, grad_feats):
     for r in range(ROWS):
         center = accum[rows_of(r + 1), :]
         if r == 0:
             center = center + from_prev[...].astype(F32)
         if r == ROWS - 1:
             center = center + from_next[...].astype(F32)
-        low = center.astype(BF16)
-        dv[rows_of(r), :] = low
-        weights = [attn[pl.ds(j * H, H), rows_of(r)] for j in range(J)]
-        terms = [grads[j][:, rows_of(r)] for j in range(J)]
-        mean = weights[0] * terms[0]
-        for j in range(1, J):
-            mean = mean + weights[j] * terms[j]
-        dl = jnp.concatenate(
-            [weights[j] * (terms[j] - mean) for j in range(J)], axis=0
-        ).astype(BF16)
-        dl_a[rows_of(r), :] = mm(dl, first, 0, 0).astype(BF16)
-        dl_b[rows_of(r), :] = mm(dl, second, 0, 0).astype(BF16)
-        out = cot[rows_of(r), :].astype(F32) + mm(low, w_value[...], 1, 1)
-        out = out + mm(dl, wl_t[...], 0, 0)
+        out = cot[rows_of(r), :].astype(F32) + mm(center.astype(BF16), w_value[...], 1, 1)
+        out = out + mm(dl_t[:, rows_of(r)], wl_t[...], 0, 0)
         grad_feats[rows_of(r), :] = out.astype(BF16)
-    core = lax.axis_index("core")
-    for mine in (0, 1):
-
-        @pl.when(core == mine)
-        def _():
-            upper, lower = (keep, send) if mine == 0 else (send, keep)
-            upper[:, pl.ds(0, C)] = gwo[...]
-            upper[:, pl.ds(C, COLS)] = mm(feats[...], dl_a[...], 0, 0)
-            lower[:, pl.ds(0, C)] = mm(feats[...], dv[...], 0, 0)
-            lower[:, pl.ds(C, COLS)] = mm(feats[...], dl_b[...], 0, 0)
 
 
 VM = pl.BlockSpec(memory_space=pltpu.VMEM)
@@ -216,14 +240,17 @@
         out_shape=(
             sds((CELLS, C), BF16),
             sds((H * J, CELLS), F32),
-            sds((K, 16, CELLS), BF16),
+            sds((CELLS + PACK, C), BF16),
+            sds((CELLS + 3 * PACK, C), BF16),
+            sds((CELLS + PACK, C), BF16),
+            sds((CELLS + PACK, C), BF16),
             sds((H, CELLS), F32),
             sds((EXT, C), F32),
             sds((C, C), F32),
             sds((H * J, C), BF16),
         ),
         in_specs=[SM] + [HB] * 8,
-        out_specs=(VM,) * 7,
+        out_specs=(VM,) * 10,
         scratch_shapes=[
             pltpu.VMEM((CELLS, C), BF16),
             pltpu.VMEM((CELLS, C), BF16),
@@ -247,34 +274,29 @@
     )
 
 
-def slot_call(cot, packet, ext, w_out, accum, gwo):
+def slot_call(cot_at, pack_at, message, ext, w_out, accum, gwo):
     return pl.pallas_call(
-        slot_body,
+        functools.partial(slot_body, cot_at, pack_at),
         name="slot",
         out_shape=(sds((H, CELLS), F32), sds((EXT, C), F32), sds((C, C), F32)),
-        in_specs=[VM] * 6,
+        in_specs=[VM] * 5,
         out_specs=(VM,) * 3,
         scratch_shapes=[pltpu.VMEM((CELLS, C), BF16)],
-        input_output_aliases={4: 1, 5: 2},
+        input_output_aliases={3: 1, 4: 2},
         compiler_params=PARAMS,
         cost_estimate=cost(10**9, 4 * 10**6),
-    )(cot, packet, ext, w_out, accum, gwo)
-
-
-def final(*args):
+    )(message, ext, w_out, accum, gwo)
+
+
+def plain(body, outs, scratch, *args):
     return pl.pallas_call(
-        final_body,
-        name="final",
-        out_shape=(sds((CELLS, C), BF16), sds((C, PAY), F32), sds((C, PAY), F32)),
-        in_specs=[VM] * 15,
-        out_specs=(VM,) * 3,
-        scratch_shapes=[
-            pltpu.VMEM((CELLS, C), BF16),
-            pltpu.VMEM((CELLS, COLS), BF16),
-            pltpu.VMEM((CELLS, COLS), BF16),
-        ],
+        body,
+        out_shape=outs,
+        in_specs=[VM] * len(args),
+        out_specs=(VM,) * len(outs),
+        scratch_shapes=scratch,
         compiler_params=PARAMS,
-        cost_estimate=cost(10**9, 4 * 10**6),
+        cost_estimate=cost(2 * 10**8, 2 * 10**6),
     )(*args)
 
 
@@ -292,49 +314,63 @@
     inputs = feats.reshape(CELLS, C)
     grad_out = cotangent.reshape(CELLS, C)
     count = size(TM)
-    cots = [None] * K
-    cots[1] = shifted(grad_out, TM, -2)
-    cots[4] = shifted(grad_out, TM, -16)
-    near = lax.ppermute(grad_out, TM, [(i, i - 1) for i in range(1, count, 2)])
-    cots[3] = shifted(grad_out, TM, -8)
-    values, attn, packets, d0, accum, gwo, wl_t = prep(
+    low = shifted(inputs[CELLS - COLS :], "band", 1)
+    high = shifted(inputs[:COLS], "band", -1)
+    values, attn, m16, m2, m1, m8, d0, accum, gwo, wl_t = prep(
         present, inputs, grad_out, w_value, w_logit.T, w_out, row_offsets[0], col_offsets[0], fractions[0]
     )
-    cots[2] = shifted(cots[1], TM, -2)
-    far = lax.ppermute(cots[1], TM, [(i, i + 1) for i in range(0, count, 2)])
-    cots[0] = near + far
-    packs = [None] * K
-    for k in SLOTS:
-        packs[k] = shifted(packets[k], TM, -DISTANCES[k])
-    low = shifted(values[CELLS - COLS :], "band", 1)
-    high = shifted(values[:COLS], "band", -1)
-    ext = jnp.concatenate([low, values, high], axis=0)
+    messages = [None] * K
+    messages[1] = shifted(m2, TM, -2)
+    messages[4] = shifted(m16, TM, -16)
+    messages[3] = shifted(m8, TM, -8)
+    near = lax.ppermute(m1, TM, [(i, i - 1) for i in range(1, count, 2)])
+    (ext,) = plain(ext_body, (sds((EXT, C), BF16),), [], values, low, high, w_value)
+    messages[2] = shifted(messages[1][: CELLS + PACK], TM, -2)
+    far = lax.ppermute(
+        messages[1][PACK : CELLS + 2 * PACK], TM, [(i, i + 1) for i in range(0, count, 2)]
+    )
+    messages[0] = near + far
+    places = ((0, CELLS), (PACK, CELLS + 2 * PACK), (PACK, 0), (0, CELLS), (0, CELLS))
     grads = [None] * K
     back = [None] * K
     for k in SLOTS:
-        grads[k], accum, gwo = slot_call(cots[k], packs[k], ext, w_out, accum, gwo)
+        grads[k], accum, gwo = slot_call(*places[k], messages[k], ext, w_out, accum, gwo)
         back[k] = shifted(grads[k], TM, DISTANCES[k])
-    from_next = shifted(accum[:COLS].astype(BF16), "band", -1)
-    from_prev = shifted(accum[EXT - COLS :].astype(BF16), "band", 1)
-    grad_feats, keep, send = final(
-        inputs, grad_out, w_value, wl_t, attn, d0, *back, accum, from_prev, from_next, gwo
-    )
     swap = [(0, 1), (1, 0)]
+    square = sds((C, C), F32)
+    keep, send = plain(
+        value_body, (square, square), [pltpu.VMEM((EXT, C), BF16)],
+        inputs, low, high, accum, gwo,
+    )
+    came = lax.ppermute(send, "core", swap)
+    dl_t, pay = plain(
+        logit_body, (sds((H * J, CELLS), BF16), sds((C, PAY), F32)),
+        [pltpu.VMEM((CELLS, COLS), BF16)],
+        inputs, attn, d0, *back, keep, came,
+    )
     both = ("pair", "band")
     count = size(both)
     share = C // count
-    part = keep + lax.ppermute(send, "core", swap)
-    pieces = lax.all_to_all(part, both, 0, 0, tiled=True)
+    pieces = lax.all_to_all(pay, both, 0, 0, tiled=True)
+    from_next = shifted(accum[:COLS].astype(BF16), "band", -1)
+    from_prev = shifted(accum[EXT - COLS :].astype(BF16), "band", 1)
     mine = jnp.sum(pieces.reshape(count, share, PAY), axis=0)
     spread = jnp.broadcast_to(mine[None], (count, share, PAY)).reshape(C, PAY)
     own = lax.all_to_all(spread, both, 0, 0, tiled=True)
+    (grad_feats,) = plain(
+        feats_body, (sds((CELLS, C), BF16),), [],
+        grad_out, w_value, wl_t, dl_t, accum, from_prev, from_next,
+    )
     other = lax.ppermute(own, "core", swap)
     first = lax.axis_index("core") == 0
-    upper = jnp.where(first, own, other)
-    lower = jnp.where(first, other, own)
-    half = H * J // 2
-    gwl = jnp.concatenate([upper[:, C : C + half], lower[:, C : C + half]], axis=1)
-    return (grad_feats.reshape(feats.shape), lower[:, :C], gwl, upper[:, :C])
+    own_square, other_square = own[:, :C], other[:, :C]
+    gwl = (own[:, C:] + other[:, C:])[:, : H * J]
+    return (
+        grad_feats.reshape(feats.shape),
+        jnp.where(first, other_square, own_square),
+        gwl,
+        jnp.where(first, own_square, other_square),
+    )
 
 
 def solution(mesh):

time: 207 us -> 188 us (0.908)
  the two profiles are of different devices: /device:TPU:1 before, /device:TPU:6 now
where the time goes in v1:
time: 188 us
  starting transfers between devices  66.2 us (35%)
  blocking collectives  52.8 us (28%)
  waiting for transfers between devices  41.1 us (22%)
  Pallas kernels  23.1 us (12%)
  local copies, waits for them, and re-layouts  2.13 us (1%)
    ppermute x13, starting transfers between devices, shifted(): lax.ppermute(value, axis, [(source, source + steps) for source in range(i...  59.5 us
    ppermute x13, waiting for transfers between devices, shifted(): lax.ppermute(value, axis, [(source, source + steps) for source in range(i...  41.1 us
    all_to_all x1, blocking collectives, layer(): pieces = lax.all_to_all(pay, both, 0, 0, tiled=True)  29.2 us
    all_to_all x1, blocking collectives, layer(): own = lax.all_to_all(spread, both, 0, 0, tiled=True)  23.6 us
    pallas_call x5, Pallas kernels, slot_call(): pl.pallas_call(functools.partial(slot_body, cot_at, pack_at), name='slot'...  15.1 us
    pallas_call x1, Pallas kernels, prep(): pl.pallas_call(prep_body, name='prep', out_shape=(sds((CELLS, C), BF16),...  5.43 us
  transfers between devices with their start and end apart: 17, of which 7 were waited for; matrix products, arithmetic and copies ran while one was open for 0% of the time, Pallas kernels for 7%

profile of v1, /device:TPU:6, one launch (start us, length us, event | category | flops | bytes accessed | tf_op | source)
XLA Modules:
  0.0 187.8 jit_solution(10795332613495378989)
XLA Ops:
  1.3 5.4 %prep.1 = (bf16[1024,256]{1,0:T(8,128)(2,1)S(1)}, f32[48,1024]{1,0:T(8,128)S(1)}, bf16[1088,256]{1,0:T(8,128)(2,1)S(1)}, bf16[1216,256]{1,0:T(8,128)(2,1)S(1)}, ...) custom-call(s32[1,5]{1,0:T(1,128)S(1)} %copy-done.4, ...), custom_call_target="tpu_custom_call" | custom-call | flops 1000000000 | bytes 4000000 | tf_op jit(solution)/shard_map/prep/pallas_call | solution.py:237
  6.7 1.4 collective-permute-start.1
  8.2 1.3 collective-permute-start.5
  9.5 1.3 collective-permute-start
  10.8 13.8 %collective-permute-done.1.message = bf16[1216,256]{1,0:T(8,128)(2,1)S(1)} collective-permute-done((bf16[1216,256]{1,0:T(8,128)(2,1)S(1)}, bf16[1216,256]{1,0:T(8,128)(2,1)S(1)}, u32[]{:S(2)}, u32[]{:S(2)}) %collective-permute-start.1) | collective-permute-done | bytes 622624 | tf_op jit(solution)/shard_map/ppermute | solution.py:310
  24.6 1.5 collective-permute-start.2
  26.1 10.8 %collective-permute-start.3 = (bf16[128,256]{1,0:T(8,128)(2,1)S(1)}, bf16[128,256]{1,0:T(8,128)(2,1)S(1)}, u32[]{:S(2)}, u32[]{:S(2)}) collective-permute-start(bf16[128,256]{1,0:T(8,128)(2,1)S(1)} %get-tuple-element.77), channel_id=1, source_target_pairs={{0,1},{1,2},{2,3},{3,4},{4,5},{5,6},{6,7},{8,9},{9,10},{10,11},{11... | collective-permute-start | bytes 196616 | tf_op jit(solution)/shard_map/ppermute | solution.py:310
  37.0 1.3 collective-permute-start.8
  38.8 1.9 %collective-permute-start.4 = (bf16[128,256]{1,0:T(8,128)(2,1)S(1)}, bf16[128,256]{1,0:T(8,128)(2,1)S(1)}, u32[]{:S(2)}, u32[]{:S(2)}) collective-permute-start(bf16[128,256]{1,0:T(8,128)(2,1)S(1)} %get-tuple-element.76), channel_id=1, source_target_pairs={{1,0},{2,1},{3,2},{4,3},{5,4},{6,5},{7,6},{9,8},{10,9},{11,10},{12... | collective-permute-start | bytes 196616 | tf_op jit(solution)/shard_map/ppermute | solution.py:310
  40.8 10.6 %collective-permute-done.4.high = bf16[128,256]{1,0:T(8,128)(2,1)S(1)} collective-permute-done((bf16[128,256]{1,0:T(8,128)(2,1)S(1)}, bf16[128,256]{1,0:T(8,128)(2,1)S(1)}, u32[]{:S(2)}, u32[]{:S(2)}) %collective-permute-start.4) | collective-permute-done | bytes 65568 | tf_op jit(solution)/shard_map/ppermute | solution.py:310
  51.4 1.5 collective-permute-start.10
  53.0 3.0 %slot.5 = (f32[8,1024]{1,0:T(8,128)S(1)}, f32[1280,256]{1,0:T(8,128)S(1)}, f32[256,256]{1,0:T(8,128)S(1)}) custom-call(bf16[1088,256]{1,0:T(8,128)(2,1)S(1)} %collective-permute-done.5.message, bf16[1280,256]{1,0:T(8,128)(2,1)S(1)} %shard_map.120.ext, bf16[256,256]{1,0:T(8,128)(2,1)S(1)} %copy-done.3, ...), custom_call_target="tpu_custom_call", output_to_operand_aliasing={{1}: (3, {}), {2}: (4, {})} | custom-call | flops 1000000000 | bytes 4000000 | tf_op jit(solution)/shard_map/slot/pallas_call | solution.py:278
  56.1 3.0 %slot.6 = (f32[8,1024]{1,0:T(8,128)S(1)}, f32[1280,256]{1,0:T(8,128)S(1)}, f32[256,256]{1,0:T(8,128)S(1)}) custom-call(bf16[1216,256]{1,0:T(8,128)(2,1)S(1)} %collective-permute-done.1.message, bf16[1280,256]{1,0:T(8,128)(2,1)S(1)} %shard_map.120.ext, bf16[256,256]{1,0:T(8,128)(2,1)S(1)} %copy-done.3, ...), custom_call_target="tpu_custom_call", output_to_operand_aliasing={{1}: (3, {}), {2}: (4, {})} | custom-call | flops 1000000000 | bytes 4000000 | tf_op jit(solution)/shard_map/slot/pallas_call | solution.py:278
  59.3 3.0 %slot.7 = (f32[8,1024]{1,0:T(8,128)S(1)}, f32[1280,256]{1,0:T(8,128)S(1)}, f32[256,256]{1,0:T(8,128)S(1)}) custom-call(bf16[1088,256]{1,0:T(8,128)(2,1)S(1)} %add.6.message, bf16[1280,256]{1,0:T(8,128)(2,1)S(1)} %shard_map.120.ext, bf16[256,256]{1,0:T(8,128)(2,1)S(1)} %copy-done.3, ...), custom_call_target="tpu_custom_call", output_to_operand_aliasing={{1}: (3, {}), {2}: (4, {})} | custom-call | flops 1000000000 | bytes 4000000 | tf_op jit(solution)/shard_map/slot/pallas_call | solution.py:278
  62.3 3.0 %slot.8 = (f32[8,1024]{1,0:T(8,128)S(1)}, f32[1280,256]{1,0:T(8,128)S(1)}, f32[256,256]{1,0:T(8,128)S(1)}) custom-call(bf16[1088,256]{1,0:T(8,128)(2,1)S(1)} %collective-permute-done.8.message, bf16[1280,256]{1,0:T(8,128)(2,1)S(1)} %shard_map.120.ext, bf16[256,256]{1,0:T(8,128)(2,1)S(1)} %copy-done.3, ...), custom_call_target="tpu_custom_call", output_to_operand_aliasing={{1}: (3, {}), {2}: (4, {})} | custom-call | flops 1000000000 | bytes 4000000 | tf_op jit(solution)/shard_map/slot/pallas_call | solution.py:278
  65.4 5.3 %collective-permute-done.10.message = bf16[1088,256]{1,0:T(8,128)(2,1)S(1)} collective-permute-done((bf16[1088,256]{1,0:T(8,128)(2,1)S(1)}, bf16[1088,256]{1,0:T(8,128)(2,1)S(1)}, u32[]{:S(2)}, u32[]{:S(2)}) %collective-permute-start.10) | collective-permute-done | bytes 557088 | tf_op jit(solution)/shard_map/ppermute | solution.py:310
  70.6 3.0 %slot.9 = (f32[8,1024]{1,0:T(8,128)S(1)}, f32[1280,256]{1,0:T(8,128)S(1)}, f32[256,256]{1,0:T(8,128)S(1)}) custom-call(bf16[1088,256]{1,0:T(8,128)(2,1)S(1)} %collective-permute-done.10.message, bf16[1280,256]{1,0:T(8,128)(2,1)S(1)} %shard_map.120.ext, bf16[256,256]{1,0:T(8,128)(2,1)S(1)} %copy-done.3, ...), custom_call_target="tpu_custom_call", output_to_operand_aliasing={{1}: (3, {}), {2}: (4, {})} | custom-call | flops 1000000000 | bytes 4000000 | tf_op jit(solution)/shard_map/slot/pallas_call | solution.py:278
  74.1 1.9 %collective-permute-start.13 = (f32[256,256]{1,0:T(8,128)S(1)}, f32[256,256]{1,0:T(8,128)S(1)}, u32[]{:S(2)}, u32[]{:S(2)}) collective-permute-start(f32[256,256]{1,0:T(8,128)S(1)} %get-tuple-element.59), channel_id=1, source_target_pairs={{0,8},{8,0},{1,9},{9,1},{2,10},{10,2},{3,11},{11,3},{4,12},{12,4},... | collective-permute-start | bytes 786440 | tf_op jit(solution)/shard_map/ppermute | solution.py:345
  76.1 18.4 %collective-permute-start.12 = (f32[8,1024]{1,0:T(8,128)S(1)}, f32[8,1024]{1,0:T(8,128)S(1)}, u32[]{:S(2)}, u32[]{:S(2)}) collective-permute-start(f32[8,1024]{1,0:T(8,128)S(1)} %get-tuple-element.55), channel_id=1, source_target_pairs={{0,128},{8,136},{16,144},{24,152},{32,160},{40,168},{48,176},{56,1... | collective-permute-start | bytes 98312 | tf_op jit(solution)/shard_map/ppermute | solution.py:310
  94.5 1.3 collective-permute-start.7
  95.8 5.1 %collective-permute-start.11 = (f32[8,1024]{1,0:T(8,128)S(1)}, f32[8,1024]{1,0:T(8,128)S(1)}, u32[]{:S(2)}, u32[]{:S(2)}) collective-permute-start(f32[8,1024]{1,0:T(8,128)S(1)} %get-tuple-element.54), channel_id=1, source_target_pairs={{0,64},{8,72},{16,80},{24,88},{32,96},{40,104},{48,112},{56,120},{... | collective-permute-start | bytes 98312 | tf_op jit(solution)/shard_map/ppermute | solution.py:310
  100.8 6.4 %collective-permute-start.9 = (f32[8,1024]{1,0:T(8,128)S(1)}, f32[8,1024]{1,0:T(8,128)S(1)}, u32[]{:S(2)}, u32[]{:S(2)}) collective-permute-start(f32[8,1024]{1,0:T(8,128)S(1)} %get-tuple-element.50), channel_id=1, source_target_pairs={{0,32},{8,40},{16,48},{24,56},{32,64},{40,72},{48,80},{56,88},{64,... | collective-permute-start | bytes 98312 | tf_op jit(solution)/shard_map/ppermute | solution.py:310
  107.3 1.5 collective-permute-start.6
  110.4 29.2 %all_to_all.18 = f32[256,1,384]{2,1,0:T(1,128)S(1)} all-to-all(f32[256,1,384]{2,1,0:T(1,128)S(1)} %copy.24), channel_id=1, replica_groups=mesh['pair'=32,'core'=2,'band'=8] {'pair','band'}, dimensions={0} | all-to-all | bytes 786432 | tf_op jit(solution)/shard_map/all_to_all | solution.py:354
  140.1 23.6 %all_to_all.19 = f32[256,1,384]{2,1,0:T(1,128)S(1)} all-to-all(f32[256,1,384]{2,1,0:T(1,128)S(1)} %reshape.38), channel_id=1, replica_groups=mesh['pair'=32,'core'=2,'band'=8] {'pair','band'}, dimensions={0} | all-to-all | bytes 786432 | tf_op jit(solution)/shard_map/all_to_all | solution.py:359
  163.7 2.1 %collective-permute-start.16 = (f32[256,384]{1,0:T(8,128)S(1)}, f32[256,384]{1,0:T(8,128)S(1)}, u32[]{:S(2)}, u32[]{:S(2)}) collective-permute-start(f32[256,384]{1,0:T(8,128)S(1)} %bitcast.21), channel_id=1, source_target_pairs={{0,8},{8,0},{1,9},{9,1},{2,10},{10,2},{3,11},{11,3},{4,12},{12,4},... | collective-permute-start | bytes 1179656 | tf_op jit(solution)/shard_map/ppermute | solution.py:364
  165.9 6.7 %collective-permute-start.14 = (bf16[128,256]{1,0:T(8,128)(2,1)S(1)}, bf16[128,256]{1,0:T(8,128)(2,1)S(1)}, u32[]{:S(2)}, u32[]{:S(2)}) collective-permute-start(bf16[128,256]{1,0:T(8,128)(2,1)S(1)} %get-tuple-element.73), channel_id=1, source_target_pairs={{0,1},{1,2},{2,3},{3,4},{4,5},{5,6},{6,7},{8,9},{9,10},{10,11},{11... | collective-permute-start | bytes 196616 | tf_op jit(solution)/shard_map/ppermute | solution.py:310
  172.5 1.9 %collective-permute-start.15 = (bf16[128,256]{1,0:T(8,128)(2,1)S(1)}, bf16[128,256]{1,0:T(8,128)(2,1)S(1)}, u32[]{:S(2)}, u32[]{:S(2)}) collective-permute-start(bf16[128,256]{1,0:T(8,128)(2,1)S(1)} %get-tuple-element.72), channel_id=1, source_target_pairs={{1,0},{2,1},{3,2},{4,3},{5,4},{6,5},{7,6},{9,8},{10,9},{11,10},{12... | collective-permute-start | bytes 196616 | tf_op jit(solution)/shard_map/ppermute | solution.py:310
  174.5 10.2 %collective-permute-done.15.from_next = bf16[128,256]{1,0:T(8,128)(2,1)S(1)} collective-permute-done((bf16[128,256]{1,0:T(8,128)(2,1)S(1)}, bf16[128,256]{1,0:T(8,128)(2,1)S(1)}, u32[]{:S(2)}, u32[]{:S(2)}) %collective-permute-start.15) | collective-permute-done | bytes 65568 | tf_op jit(solution)/shard_map/ppermute | solution.py:310
  184.8 1.4 shard_map.123
  186.3 0.7 copy.25
  187.0 0.8 slice_select_fusion
  (38 shorter events, 4.4 us)
Async XLA Ops:
  0.6 0.7 copy-start.4
  6.7 19.4 %copy-start = (bf16[1,8,128,256]{3,2,1,0:T(8,128)(2,1)S(1)}, bf16[1,8,128,256]{3,2,1,0:T(8,128)(2,1)}, u32[]{:S(2)}) copy-start(bf16[1,8,128,256]{3,2,1,0:T(8,128)(2,1)} %param.9) | copy-start | bytes 1572868
  6.7 46.1 %copy-start.2 = (bf16[256,256]{1,0:T(8,128)(2,1)S(1)}, bf16[256,256]{1,0:T(8,128)(2,1)}, u32[]{:S(2)}) copy-start(bf16[256,256]{1,0:T(8,128)(2,1)} %w_value.3) | copy-start | bytes 393220
  6.7 17.8 %collective-permute-start.1 = (bf16[1216,256]{1,0:T(8,128)(2,1)S(1)}, bf16[1216,256]{1,0:T(8,128)(2,1)S(1)}, u32[]{:S(2)}, u32[]{:S(2)}) collective-permute-start(bf16[1216,256]{1,0:T(8,128)(2,1)S(1)} %get-tuple-element.37), channel_id=1, source_target_pairs={{16,0},{24,8},{32,16},{40,24},{48,32},{56,40},{64,48},{72,56},{80,... | collective-permute-start | bytes 1867784 | tf_op jit(solution)/shard_map/ppermute | solution.py:310
  8.2 44.9 %collective-permute-start.5 = (bf16[1088,256]{1,0:T(8,128)(2,1)S(1)}, bf16[1088,256]{1,0:T(8,128)(2,1)S(1)}, u32[]{:S(2)}, u32[]{:S(2)}) collective-permute-start(bf16[1088,256]{1,0:T(8,128)(2,1)S(1)} %get-tuple-element.39), channel_id=1, source_target_pairs={{128,0},{136,8},{144,16},{152,24},{160,32},{168,40},{176,48},{184,... | collective-permute-start | bytes 1671176 | tf_op jit(solution)/shard_map/ppermute | solution.py:310
  9.5 49.6 %collective-permute-start = (bf16[1088,256]{1,0:T(8,128)(2,1)S(1)}, bf16[1088,256]{1,0:T(8,128)(2,1)S(1)}, u32[]{:S(2)}, u32[]{:S(2)}) collective-permute-start(bf16[1088,256]{1,0:T(8,128)(2,1)S(1)} %get-tuple-element.36), channel_id=1, source_target_pairs={{8,0},{24,16},{40,32},{56,48},{72,64},{88,80},{104,96},{120,112},{... | collective-permute-start | bytes 1671176 | tf_op jit(solution)/shard_map/ppermute | solution.py:326
  24.6 28.4 %copy-start.3 = (bf16[256,256]{1,0:T(8,128)(2,1)S(1)}, bf16[256,256]{1,0:T(8,128)(2,1)}, u32[]{:S(2)}) copy-start(bf16[256,256]{1,0:T(8,128)(2,1)} %w_out.9) | copy-start | bytes 393220
  24.6 34.5 %collective-permute-start.2 = (bf16[1088,256]{1,0:T(8,128)(2,1)S(1)}, bf16[1088,256]{1,0:T(8,128)(2,1)S(1)}, u32[]{:S(2)}, u32[]{:S(2)}) collective-permute-start(bf16[1088,256]{1,0:T(8,128)(2,1)S(1)} %get-tuple-element.75), channel_id=1, source_target_pairs={{0,8},{16,24},{32,40},{48,56},{64,72},{80,88},{96,104},{112,120},{... | collective-permute-start | bytes 1671176 | tf_op jit(solution)/shard_map/ppermute | solution.py:329
  26.1 12.7 %collective-permute-start.3 = (bf16[128,256]{1,0:T(8,128)(2,1)S(1)}, bf16[128,256]{1,0:T(8,128)(2,1)S(1)}, u32[]{:S(2)}, u32[]{:S(2)}) collective-permute-start(bf16[128,256]{1,0:T(8,128)(2,1)S(1)} %get-tuple-element.77), channel_id=1, source_target_pairs={{0,1},{1,2},{2,3},{3,4},{4,5},{5,6},{6,7},{8,9},{9,10},{10,11},{11... | collective-permute-start | bytes 196616 | tf_op jit(solution)/shard_map/ppermute | solution.py:310
  37.0 25.4 %collective-permute-start.8 = (bf16[1088,256]{1,0:T(8,128)(2,1)S(1)}, bf16[1088,256]{1,0:T(8,128)(2,1)S(1)}, u32[]{:S(2)}, u32[]{:S(2)}) collective-permute-start(bf16[1088,256]{1,0:T(8,128)(2,1)S(1)} %get-tuple-element.74), channel_id=1, source_target_pairs={{16,0},{24,8},{32,16},{40,24},{48,32},{56,40},{64,48},{72,56},{80,... | collective-permute-start | bytes 1671176 | tf_op jit(solution)/shard_map/ppermute | solution.py:310
  38.8 12.5 %collective-permute-start.4 = (bf16[128,256]{1,0:T(8,128)(2,1)S(1)}, bf16[128,256]{1,0:T(8,128)(2,1)S(1)}, u32[]{:S(2)}, u32[]{:S(2)}) collective-permute-start(bf16[128,256]{1,0:T(8,128)(2,1)S(1)} %get-tuple-element.76), channel_id=1, source_target_pairs={{1,0},{2,1},{3,2},{4,3},{5,4},{6,5},{7,6},{9,8},{10,9},{11,10},{12... | collective-permute-start | bytes 196616 | tf_op jit(solution)/shard_map/ppermute | solution.py:310
  51.4 19.3 %collective-permute-start.10 = (bf16[1088,256]{1,0:T(8,128)(2,1)S(1)}, bf16[1088,256]{1,0:T(8,128)(2,1)S(1)}, u32[]{:S(2)}, u32[]{:S(2)}) collective-permute-start(bf16[1088,256]{1,0:T(8,128)(2,1)S(1)} %get-tuple-element.51), channel_id=1, source_target_pairs={{64,0},{72,8},{80,16},{88,24},{96,32},{104,40},{112,48},{120,56},{... | collective-permute-start | bytes 1671176 | tf_op jit(solution)/shard_map/ppermute | solution.py:310
  74.1 35.3 %collective-permute-start.13 = (f32[256,256]{1,0:T(8,128)S(1)}, f32[256,256]{1,0:T(8,128)S(1)}, u32[]{:S(2)}, u32[]{:S(2)}) collective-permute-start(f32[256,256]{1,0:T(8,128)S(1)} %get-tuple-element.59), channel_id=1, source_target_pairs={{0,8},{8,0},{1,9},{9,1},{2,10},{10,2},{3,11},{11,3},{4,12},{12,4},... | collective-permute-start | bytes 786440 | tf_op jit(solution)/shard_map/ppermute | solution.py:345
  76.1 31.2 %collective-permute-start.12 = (f32[8,1024]{1,0:T(8,128)S(1)}, f32[8,1024]{1,0:T(8,128)S(1)}, u32[]{:S(2)}, u32[]{:S(2)}) collective-permute-start(f32[8,1024]{1,0:T(8,128)S(1)} %get-tuple-element.55), channel_id=1, source_target_pairs={{0,128},{8,136},{16,144},{24,152},{32,160},{40,168},{48,176},{56,1... | collective-permute-start | bytes 98312 | tf_op jit(solution)/shard_map/ppermute | solution.py:310
  94.5 14.3 %collective-permute-start.7 = (f32[8,1024]{1,0:T(8,128)S(1)}, f32[8,1024]{1,0:T(8,128)S(1)}, u32[]{:S(2)}, u32[]{:S(2)}) collective-permute-start(f32[8,1024]{1,0:T(8,128)S(1)} %get-tuple-element.47), channel_id=1, source_target_pairs={{0,16},{8,24},{16,32},{24,40},{32,48},{40,56},{48,64},{56,72},{64,... | collective-permute-start | bytes 98312 | tf_op jit(solution)/shard_map/ppermute | solution.py:310
  95.8 13.1 %collective-permute-start.11 = (f32[8,1024]{1,0:T(8,128)S(1)}, f32[8,1024]{1,0:T(8,128)S(1)}, u32[]{:S(2)}, u32[]{:S(2)}) collective-permute-start(f32[8,1024]{1,0:T(8,128)S(1)} %get-tuple-element.54), channel_id=1, source_target_pairs={{0,64},{8,72},{16,80},{24,88},{32,96},{40,104},{48,112},{56,120},{... | collective-permute-start | bytes 98312 | tf_op jit(solution)/shard_map/ppermute | solution.py:310
  100.8 8.0 %collective-permute-start.9 = (f32[8,1024]{1,0:T(8,128)S(1)}, f32[8,1024]{1,0:T(8,128)S(1)}, u32[]{:S(2)}, u32[]{:S(2)}) collective-permute-start(f32[8,1024]{1,0:T(8,128)S(1)} %get-tuple-element.50), channel_id=1, source_target_pairs={{0,32},{8,40},{16,48},{24,56},{32,64},{40,72},{48,80},{56,88},{64,... | collective-permute-start | bytes 98312 | tf_op jit(solution)/shard_map/ppermute | solution.py:310
  107.3 2.1 %collective-permute-start.6 = (f32[8,1024]{1,0:T(8,128)S(1)}, f32[8,1024]{1,0:T(8,128)S(1)}, u32[]{:S(2)}, u32[]{:S(2)}) collective-permute-start(f32[8,1024]{1,0:T(8,128)S(1)} %get-tuple-element.46), channel_id=1, source_target_pairs={{0,8},{8,16},{16,24},{24,32},{32,40},{40,48},{48,56},{56,64},{64,7... | collective-permute-start | bytes 98312 | tf_op jit(solution)/shard_map/ppermute | solution.py:310
  163.7 21.1 %copy-start.1 = (bf16[1,8,128,256]{3,2,1,0:T(8,128)(2,1)S(1)}, bf16[1,8,128,256]{3,2,1,0:T(8,128)(2,1)}, u32[]{:S(2)}) copy-start(bf16[1,8,128,256]{3,2,1,0:T(8,128)(2,1)} %param.10) | copy-start | bytes 1572868
  163.7 22.5 %collective-permute-start.16 = (f32[256,384]{1,0:T(8,128)S(1)}, f32[256,384]{1,0:T(8,128)S(1)}, u32[]{:S(2)}, u32[]{:S(2)}) collective-permute-start(f32[256,384]{1,0:T(8,128)S(1)} %bitcast.21), channel_id=1, source_target_pairs={{0,8},{8,0},{1,9},{9,1},{2,10},{10,2},{3,11},{11,3},{4,12},{12,4},... | collective-permute-start | bytes 1179656 | tf_op jit(solution)/shard_map/ppermute | solution.py:364
  165.9 8.7 %collective-permute-start.14 = (bf16[128,256]{1,0:T(8,128)(2,1)S(1)}, bf16[128,256]{1,0:T(8,128)(2,1)S(1)}, u32[]{:S(2)}, u32[]{:S(2)}) collective-permute-start(bf16[128,256]{1,0:T(8,128)(2,1)S(1)} %get-tuple-element.73), channel_id=1, source_target_pairs={{0,1},{1,2},{2,3},{3,4},{4,5},{5,6},{6,7},{8,9},{9,10},{10,11},{11... | collective-permute-start | bytes 196616 | tf_op jit(solution)/shard_map/ppermute | solution.py:310
  172.5 12.2 %collective-permute-start.15 = (bf16[128,256]{1,0:T(8,128)(2,1)S(1)}, bf16[128,256]{1,0:T(8,128)(2,1)S(1)}, u32[]{:S(2)}, u32[]{:S(2)}) collective-permute-start(bf16[128,256]{1,0:T(8,128)(2,1)S(1)} %get-tuple-element.72), channel_id=1, source_target_pairs={{1,0},{2,1},{3,2},{4,3},{5,4},{6,5},{7,6},{9,8},{10,9},{11,10},{12... | collective-permute-start | bytes 196616 | tf_op jit(solution)/shard_map/ppermute | solution.py:310

commit v2 on v1

--- a/solution.py
+++ b/solution.py
@@ -171,11 +171,13 @@
     gwo[...] = gwo_in[...] + mm(mix[...], message[pl.ds(cot_at, CELLS), :], 0, 0)
 
 
-def value_body(feats, low, high, accum, gwo, keep, send, dv):
+def value_body(feats, low, high, accum, gwo, keep, send, rim_low, rim_high, dv):
     dv[...] = accum[...].astype(BF16)
     gwv = mm(feats[...], dv[pl.ds(COLS, CELLS), :], 0, 0)
     gwv = gwv + mm(low[...], dv[pl.ds(0, COLS), :], 0, 0)
     gwv = gwv + mm(high[...], dv[pl.ds(COLS + CELLS, COLS), :], 0, 0)
+    rim_low[...] = dv[pl.ds(0, COLS), :]
+    rim_high[...] = dv[pl.ds(COLS + CELLS, COLS), :]
     core = lax.axis_index("core")
     for mine in (0, 1):
 
@@ -338,8 +340,9 @@
         back[k] = shifted(grads[k], TM, DISTANCES[k])
     swap = [(0, 1), (1, 0)]
     square = sds((C, C), F32)
-    keep, send = plain(
-        value_body, (square, square), [pltpu.VMEM((EXT, C), BF16)],
+    rim = sds((COLS, C), BF16)
+    keep, send, rim_low, rim_high = plain(
+        value_body, (square, square, rim, rim), [pltpu.VMEM((EXT, C), BF16)],
         inputs, low, high, accum, gwo,
     )
     came = lax.ppermute(send, "core", swap)
@@ -352,8 +355,8 @@
     count = size(both)
     share = C // count
     pieces = lax.all_to_all(pay, both, 0, 0, tiled=True)
-    from_next = shifted(accum[:COLS].astype(BF16), "band", -1)
-    from_prev = shifted(accum[EXT - COLS :].astype(BF16), "band", 1)
+    from_next = shifted(rim_low, "band", -1)
+    from_prev = shifted(rim_high, "band", 1)
     mine = jnp.sum(pieces.reshape(count, share, PAY), axis=0)
     spread = jnp.broadcast_to(mine[None], (count, share, PAY)).reshape(C, PAY)
     own = lax.all_to_all(spread, both, 0, 0, tiled=True)

time: 188 us -> 188 us (level)
  no operation moved by 1% of the time
where the time goes in v2:
time: 188 us
  starting transfers between devices  66.1 us (35%)
  blocking collectives  52.7 us (28%)
  waiting for transfers between devices  41.1 us (22%)
  Pallas kernels  23.1 us (12%)
  local copies, waits for them, and re-layouts  2.11 us (1%)
    ppermute x13, starting transfers between devices, shifted(): lax.ppermute(value, axis, [(source, source + steps) for source in range(i...  59.5 us
    ppermute x13, waiting for transfers between devices, shifted(): lax.ppermute(value, axis, [(source, source + steps) for source in range(i...  41.1 us
    all_to_all x1, blocking collectives, layer(): pieces = lax.all_to_all(pay, both, 0, 0, tiled=True)  29.2 us
    all_to_all x1, blocking collectives, layer(): own = lax.all_to_all(spread, both, 0, 0, tiled=True)  23.6 us
    pallas_call x5, Pallas kernels, slot_call(): pl.pallas_call(functools.partial(slot_body, cot_at, pack_at), name='slot'...  15.1 us
    pallas_call x1, Pallas kernels, prep(): pl.pallas_call(prep_body, name='prep', out_shape=(sds((CELLS, C), BF16),...  5.43 us
  transfers between devices with their start and end apart: 17, of which 7 were waited for; matrix products, arithmetic and copies ran while one was open for 0% of the time, Pallas kernels for 7%

profile of v2, /device:TPU:6, one launch (start us, length us, event | category | flops | bytes accessed | tf_op | source)
XLA Modules:
  0.0 187.6 jit_solution(18329871542034793990)
XLA Ops:
  1.3 5.4 %prep.1 = (bf16[1024,256]{1,0:T(8,128)(2,1)S(1)}, f32[48,1024]{1,0:T(8,128)S(1)}, bf16[1088,256]{1,0:T(8,128)(2,1)S(1)}, bf16[1216,256]{1,0:T(8,128)(2,1)S(1)}, ...) custom-call(s32[1,5]{1,0:T(1,128)S(1)} %copy-done.4, ...), custom_call_target="tpu_custom_call" | custom-call | flops 1000000000 | bytes 4000000 | tf_op jit(solution)/shard_map/prep/pallas_call | solution.py:239
  6.7 1.4 collective-permute-start.1
  8.2 1.3 collective-permute-start.5
  9.5 1.3 collective-permute-start
  10.8 13.8 %collective-permute-done.1.message = bf16[1216,256]{1,0:T(8,128)(2,1)S(1)} collective-permute-done((bf16[1216,256]{1,0:T(8,128)(2,1)S(1)}, bf16[1216,256]{1,0:T(8,128)(2,1)S(1)}, u32[]{:S(2)}, u32[]{:S(2)}) %collective-permute-start.1) | collective-permute-done | bytes 622624 | tf_op jit(solution)/shard_map/ppermute | solution.py:312
  24.6 1.5 collective-permute-start.2
  26.1 10.8 %collective-permute-start.3 = (bf16[128,256]{1,0:T(8,128)(2,1)S(1)}, bf16[128,256]{1,0:T(8,128)(2,1)S(1)}, u32[]{:S(2)}, u32[]{:S(2)}) collective-permute-start(bf16[128,256]{1,0:T(8,128)(2,1)S(1)} %get-tuple-element.79), channel_id=1, source_target_pairs={{0,1},{1,2},{2,3},{3,4},{4,5},{5,6},{6,7},{8,9},{9,10},{10,11},{11... | collective-permute-start | bytes 196616 | tf_op jit(solution)/shard_map/ppermute | solution.py:312
  37.0 1.3 collective-permute-start.8
  38.8 1.9 %collective-permute-start.4 = (bf16[128,256]{1,0:T(8,128)(2,1)S(1)}, bf16[128,256]{1,0:T(8,128)(2,1)S(1)}, u32[]{:S(2)}, u32[]{:S(2)}) collective-permute-start(bf16[128,256]{1,0:T(8,128)(2,1)S(1)} %get-tuple-element.78), channel_id=1, source_target_pairs={{1,0},{2,1},{3,2},{4,3},{5,4},{6,5},{7,6},{9,8},{10,9},{11,10},{12... | collective-permute-start | bytes 196616 | tf_op jit(solution)/shard_map/ppermute | solution.py:312
  40.8 10.6 %collective-permute-done.4.high = bf16[128,256]{1,0:T(8,128)(2,1)S(1)} collective-permute-done((bf16[128,256]{1,0:T(8,128)(2,1)S(1)}, bf16[128,256]{1,0:T(8,128)(2,1)S(1)}, u32[]{:S(2)}, u32[]{:S(2)}) %collective-permute-start.4) | collective-permute-done | bytes 65568 | tf_op jit(solution)/shard_map/ppermute | solution.py:312
  51.4 1.5 collective-permute-start.10
  53.0 3.0 %slot.5 = (f32[8,1024]{1,0:T(8,128)S(1)}, f32[1280,256]{1,0:T(8,128)S(1)}, f32[256,256]{1,0:T(8,128)S(1)}) custom-call(bf16[1088,256]{1,0:T(8,128)(2,1)S(1)} %collective-permute-done.5.message, bf16[1280,256]{1,0:T(8,128)(2,1)S(1)} %shard_map.120.ext, bf16[256,256]{1,0:T(8,128)(2,1)S(1)} %copy-done.3, ...), custom_call_target="tpu_custom_call", output_to_operand_aliasing={{1}: (3, {}), {2}: (4, {})} | custom-call | flops 1000000000 | bytes 4000000 | tf_op jit(solution)/shard_map/slot/pallas_call | solution.py:280
  56.1 3.0 %slot.6 = (f32[8,1024]{1,0:T(8,128)S(1)}, f32[1280,256]{1,0:T(8,128)S(1)}, f32[256,256]{1,0:T(8,128)S(1)}) custom-call(bf16[1216,256]{1,0:T(8,128)(2,1)S(1)} %collective-permute-done.1.message, bf16[1280,256]{1,0:T(8,128)(2,1)S(1)} %shard_map.120.ext, bf16[256,256]{1,0:T(8,128)(2,1)S(1)} %copy-done.3, ...), custom_call_target="tpu_custom_call", output_to_operand_aliasing={{1}: (3, {}), {2}: (4, {})} | custom-call | flops 1000000000 | bytes 4000000 | tf_op jit(solution)/shard_map/slot/pallas_call | solution.py:280
  59.3 3.0 %slot.7 = (f32[8,1024]{1,0:T(8,128)S(1)}, f32[1280,256]{1,0:T(8,128)S(1)}, f32[256,256]{1,0:T(8,128)S(1)}) custom-call(bf16[1088,256]{1,0:T(8,128)(2,1)S(1)} %add.6.message, bf16[1280,256]{1,0:T(8,128)(2,1)S(1)} %shard_map.120.ext, bf16[256,256]{1,0:T(8,128)(2,1)S(1)} %copy-done.3, ...), custom_call_target="tpu_custom_call", output_to_operand_aliasing={{1}: (3, {}), {2}: (4, {})} | custom-call | flops 1000000000 | bytes 4000000 | tf_op jit(solution)/shard_map/slot/pallas_call | solution.py:280
  62.3 3.0 %slot.8 = (f32[8,1024]{1,0:T(8,128)S(1)}, f32[1280,256]{1,0:T(8,128)S(1)}, f32[256,256]{1,0:T(8,128)S(1)}) custom-call(bf16[1088,256]{1,0:T(8,128)(2,1)S(1)} %collective-permute-done.8.message, bf16[1280,256]{1,0:T(8,128)(2,1)S(1)} %shard_map.120.ext, bf16[256,256]{1,0:T(8,128)(2,1)S(1)} %copy-done.3, ...), custom_call_target="tpu_custom_call", output_to_operand_aliasing={{1}: (3, {}), {2}: (4, {})} | custom-call | flops 1000000000 | bytes 4000000 | tf_op jit(solution)/shard_map/slot/pallas_call | solution.py:280
  65.4 5.3 %collective-permute-done.10.message = bf16[1088,256]{1,0:T(8,128)(2,1)S(1)} collective-permute-done((bf16[1088,256]{1,0:T(8,128)(2,1)S(1)}, bf16[1088,256]{1,0:T(8,128)(2,1)S(1)}, u32[]{:S(2)}, u32[]{:S(2)}) %collective-permute-start.10) | collective-permute-done | bytes 557088 | tf_op jit(solution)/shard_map/ppermute | solution.py:312
  70.6 3.0 %slot.9 = (f32[8,1024]{1,0:T(8,128)S(1)}, f32[1280,256]{1,0:T(8,128)S(1)}, f32[256,256]{1,0:T(8,128)S(1)}) custom-call(bf16[1088,256]{1,0:T(8,128)(2,1)S(1)} %collective-permute-done.10.message, bf16[1280,256]{1,0:T(8,128)(2,1)S(1)} %shard_map.120.ext, bf16[256,256]{1,0:T(8,128)(2,1)S(1)} %copy-done.3, ...), custom_call_target="tpu_custom_call", output_to_operand_aliasing={{1}: (3, {}), {2}: (4, {})} | custom-call | flops 1000000000 | bytes 4000000 | tf_op jit(solution)/shard_map/slot/pallas_call | solution.py:280
  74.1 1.9 %collective-permute-start.13 = (f32[256,256]{1,0:T(8,128)S(1)}, f32[256,256]{1,0:T(8,128)S(1)}, u32[]{:S(2)}, u32[]{:S(2)}) collective-permute-start(f32[256,256]{1,0:T(8,128)S(1)} %get-tuple-element.61), channel_id=1, source_target_pairs={{0,8},{8,0},{1,9},{9,1},{2,10},{10,2},{3,11},{11,3},{4,12},{12,4},... | collective-permute-start | bytes 786440 | tf_op jit(solution)/shard_map/ppermute | solution.py:348
  76.1 18.4 %collective-permute-start.12 = (f32[8,1024]{1,0:T(8,128)S(1)}, f32[8,1024]{1,0:T(8,128)S(1)}, u32[]{:S(2)}, u32[]{:S(2)}) collective-permute-start(f32[8,1024]{1,0:T(8,128)S(1)} %get-tuple-element.57), channel_id=1, source_target_pairs={{0,128},{8,136},{16,144},{24,152},{32,160},{40,168},{48,176},{56,1... | collective-permute-start | bytes 98312 | tf_op jit(solution)/shard_map/ppermute | solution.py:312
  94.5 1.3 collective-permute-start.7
  95.8 5.1 %collective-permute-start.11 = (f32[8,1024]{1,0:T(8,128)S(1)}, f32[8,1024]{1,0:T(8,128)S(1)}, u32[]{:S(2)}, u32[]{:S(2)}) collective-permute-start(f32[8,1024]{1,0:T(8,128)S(1)} %get-tuple-element.56), channel_id=1, source_target_pairs={{0,64},{8,72},{16,80},{24,88},{32,96},{40,104},{48,112},{56,120},{... | collective-permute-start | bytes 98312 | tf_op jit(solution)/shard_map/ppermute | solution.py:312
  100.8 6.4 %collective-permute-start.9 = (f32[8,1024]{1,0:T(8,128)S(1)}, f32[8,1024]{1,0:T(8,128)S(1)}, u32[]{:S(2)}, u32[]{:S(2)}) collective-permute-start(f32[8,1024]{1,0:T(8,128)S(1)} %get-tuple-element.52), channel_id=1, source_target_pairs={{0,32},{8,40},{16,48},{24,56},{32,64},{40,72},{48,80},{56,88},{64,... | collective-permute-start | bytes 98312 | tf_op jit(solution)/shard_map/ppermute | solution.py:312
  107.3 1.5 collective-permute-start.6
  110.4 29.2 %all_to_all.18 = f32[256,1,384]{2,1,0:T(1,128)S(1)} all-to-all(f32[256,1,384]{2,1,0:T(1,128)S(1)} %copy.24), channel_id=1, replica_groups=mesh['pair'=32,'core'=2,'band'=8] {'pair','band'}, dimensions={0} | all-to-all | bytes 786432 | tf_op jit(solution)/shard_map/all_to_all | solution.py:357
  140.1 23.6 %all_to_all.19 = f32[256,1,384]{2,1,0:T(1,128)S(1)} all-to-all(f32[256,1,384]{2,1,0:T(1,128)S(1)} %reshape.38), channel_id=1, replica_groups=mesh['pair'=32,'core'=2,'band'=8] {'pair','band'}, dimensions={0} | all-to-all | bytes 786432 | tf_op jit(solution)/shard_map/all_to_all | solution.py:362
  163.7 1.9 %collective-permute-start.16 = (f32[256,384]{1,0:T(8,128)S(1)}, f32[256,384]{1,0:T(8,128)S(1)}, u32[]{:S(2)}, u32[]{:S(2)}) collective-permute-start(f32[256,384]{1,0:T(8,128)S(1)} %bitcast.21), channel_id=1, source_target_pairs={{0,8},{8,0},{1,9},{9,1},{2,10},{10,2},{3,11},{11,3},{4,12},{12,4},... | collective-permute-start | bytes 1179656 | tf_op jit(solution)/shard_map/ppermute | solution.py:367
  165.6 6.7 %collective-permute-start.14 = (bf16[128,256]{1,0:T(8,128)(2,1)S(1)}, bf16[128,256]{1,0:T(8,128)(2,1)S(1)}, u32[]{:S(2)}, u32[]{:S(2)}) collective-permute-start(bf16[128,256]{1,0:T(8,128)(2,1)S(1)} %get-tuple-element.63), channel_id=1, source_target_pairs={{0,1},{1,2},{2,3},{3,4},{4,5},{5,6},{6,7},{8,9},{9,10},{10,11},{11... | collective-permute-start | bytes 196616 | tf_op jit(solution)/shard_map/ppermute | solution.py:312
  172.3 1.9 %collective-permute-start.15 = (bf16[128,256]{1,0:T(8,128)(2,1)S(1)}, bf16[128,256]{1,0:T(8,128)(2,1)S(1)}, u32[]{:S(2)}, u32[]{:S(2)}) collective-permute-start(bf16[128,256]{1,0:T(8,128)(2,1)S(1)} %get-tuple-element.64), channel_id=1, source_target_pairs={{1,0},{2,1},{3,2},{4,3},{5,4},{6,5},{7,6},{9,8},{10,9},{11,10},{12... | collective-permute-start | bytes 196616 | tf_op jit(solution)/shard_map/ppermute | solution.py:312
  174.3 10.2 %collective-permute-done.15.from_next = bf16[128,256]{1,0:T(8,128)(2,1)S(1)} collective-permute-done((bf16[128,256]{1,0:T(8,128)(2,1)S(1)}, bf16[128,256]{1,0:T(8,128)(2,1)S(1)}, u32[]{:S(2)}, u32[]{:S(2)}) %collective-permute-start.15) | collective-permute-done | bytes 65568 | tf_op jit(solution)/shard_map/ppermute | solution.py:312
  184.5 1.4 shard_map.123
  186.0 0.7 copy.25
  186.7 0.8 slice_select_fusion
  (36 shorter events, 4.3 us)
Async XLA Ops:
  0.6 0.7 copy-start.4
  6.7 19.4 %copy-start = (bf16[1,8,128,256]{3,2,1,0:T(8,128)(2,1)S(1)}, bf16[1,8,128,256]{3,2,1,0:T(8,128)(2,1)}, u32[]{:S(2)}) copy-start(bf16[1,8,128,256]{3,2,1,0:T(8,128)(2,1)} %param.9) | copy-start | bytes 1572868
  6.7 46.1 %copy-start.2 = (bf16[256,256]{1,0:T(8,128)(2,1)S(1)}, bf16[256,256]{1,0:T(8,128)(2,1)}, u32[]{:S(2)}) copy-start(bf16[256,256]{1,0:T(8,128)(2,1)} %w_value.3) | copy-start | bytes 393220
  6.7 17.8 %collective-permute-start.1 = (bf16[1216,256]{1,0:T(8,128)(2,1)S(1)}, bf16[1216,256]{1,0:T(8,128)(2,1)S(1)}, u32[]{:S(2)}, u32[]{:S(2)}) collective-permute-start(bf16[1216,256]{1,0:T(8,128)(2,1)S(1)} %get-tuple-element.39), channel_id=1, source_target_pairs={{16,0},{24,8},{32,16},{40,24},{48,32},{56,40},{64,48},{72,56},{80,... | collective-permute-start | bytes 1867784 | tf_op jit(solution)/shard_map/ppermute | solution.py:312
  8.2 44.9 %collective-permute-start.5 = (bf16[1088,256]{1,0:T(8,128)(2,1)S(1)}, bf16[1088,256]{1,0:T(8,128)(2,1)S(1)}, u32[]{:S(2)}, u32[]{:S(2)}) collective-permute-start(bf16[1088,256]{1,0:T(8,128)(2,1)S(1)} %get-tuple-element.41), channel_id=1, source_target_pairs={{128,0},{136,8},{144,16},{152,24},{160,32},{168,40},{176,48},{184,... | collective-permute-start | bytes 1671176 | tf_op jit(solution)/shard_map/ppermute | solution.py:312
  9.5 49.6 %collective-permute-start = (bf16[1088,256]{1,0:T(8,128)(2,1)S(1)}, bf16[1088,256]{1,0:T(8,128)(2,1)S(1)}, u32[]{:S(2)}, u32[]{:S(2)}) collective-permute-start(bf16[1088,256]{1,0:T(8,128)(2,1)S(1)} %get-tuple-element.38), channel_id=1, source_target_pairs={{8,0},{24,16},{40,32},{56,48},{72,64},{88,80},{104,96},{120,112},{... | collective-permute-start | bytes 1671176 | tf_op jit(solution)/shard_map/ppermute | solution.py:328
  24.6 28.4 %copy-start.3 = (bf16[256,256]{1,0:T(8,128)(2,1)S(1)}, bf16[256,256]{1,0:T(8,128)(2,1)}, u32[]{:S(2)}) copy-start(bf16[256,256]{1,0:T(8,128)(2,1)} %w_out.9) | copy-start | bytes 393220
  24.6 34.5 %collective-permute-start.2 = (bf16[1088,256]{1,0:T(8,128)(2,1)S(1)}, bf16[1088,256]{1,0:T(8,128)(2,1)S(1)}, u32[]{:S(2)}, u32[]{:S(2)}) collective-permute-start(bf16[1088,256]{1,0:T(8,128)(2,1)S(1)} %get-tuple-element.77), channel_id=1, source_target_pairs={{0,8},{16,24},{32,40},{48,56},{64,72},{80,88},{96,104},{112,120},{... | collective-permute-start | bytes 1671176 | tf_op jit(solution)/shard_map/ppermute | solution.py:331
  26.1 12.7 %collective-permute-start.3 = (bf16[128,256]{1,0:T(8,128)(2,1)S(1)}, bf16[128,256]{1,0:T(8,128)(2,1)S(1)}, u32[]{:S(2)}, u32[]{:S(2)}) collective-permute-start(bf16[128,256]{1,0:T(8,128)(2,1)S(1)} %get-tuple-element.79), channel_id=1, source_target_pairs={{0,1},{1,2},{2,3},{3,4},{4,5},{5,6},{6,7},{8,9},{9,10},{10,11},{11... | collective-permute-start | bytes 196616 | tf_op jit(solution)/shard_map/ppermute | solution.py:312
  37.0 25.4 %collective-permute-start.8 = (bf16[1088,256]{1,0:T(8,128)(2,1)S(1)}, bf16[1088,256]{1,0:T(8,128)(2,1)S(1)}, u32[]{:S(2)}, u32[]{:S(2)}) collective-permute-start(bf16[1088,256]{1,0:T(8,128)(2,1)S(1)} %get-tuple-element.76), channel_id=1, source_target_pairs={{16,0},{24,8},{32,16},{40,24},{48,32},{56,40},{64,48},{72,56},{80,... | collective-permute-start | bytes 1671176 | tf_op jit(solution)/shard_map/ppermute | solution.py:312
  38.8 12.5 %collective-permute-start.4 = (bf16[128,256]{1,0:T(8,128)(2,1)S(1)}, bf16[128,256]{1,0:T(8,128)(2,1)S(1)}, u32[]{:S(2)}, u32[]{:S(2)}) collective-permute-start(bf16[128,256]{1,0:T(8,128)(2,1)S(1)} %get-tuple-element.78), channel_id=1, source_target_pairs={{1,0},{2,1},{3,2},{4,3},{5,4},{6,5},{7,6},{9,8},{10,9},{11,10},{12... | collective-permute-start | bytes 196616 | tf_op jit(solution)/shard_map/ppermute | solution.py:312
  51.4 19.3 %collective-permute-start.10 = (bf16[1088,256]{1,0:T(8,128)(2,1)S(1)}, bf16[1088,256]{1,0:T(8,128)(2,1)S(1)}, u32[]{:S(2)}, u32[]{:S(2)}) collective-permute-start(bf16[1088,256]{1,0:T(8,128)(2,1)S(1)} %get-tuple-element.53), channel_id=1, source_target_pairs={{64,0},{72,8},{80,16},{88,24},{96,32},{104,40},{112,48},{120,56},{... | collective-permute-start | bytes 1671176 | tf_op jit(solution)/shard_map/ppermute | solution.py:312
  74.1 35.3 %collective-permute-start.13 = (f32[256,256]{1,0:T(8,128)S(1)}, f32[256,256]{1,0:T(8,128)S(1)}, u32[]{:S(2)}, u32[]{:S(2)}) collective-permute-start(f32[256,256]{1,0:T(8,128)S(1)} %get-tuple-element.61), channel_id=1, source_target_pairs={{0,8},{8,0},{1,9},{9,1},{2,10},{10,2},{3,11},{11,3},{4,12},{12,4},... | collective-permute-start | bytes 786440 | tf_op jit(solution)/shard_map/ppermute | solution.py:348
  76.1 31.2 %collective-permute-start.12 = (f32[8,1024]{1,0:T(8,128)S(1)}, f32[8,1024]{1,0:T(8,128)S(1)}, u32[]{:S(2)}, u32[]{:S(2)}) collective-permute-start(f32[8,1024]{1,0:T(8,128)S(1)} %get-tuple-element.57), channel_id=1, source_target_pairs={{0,128},{8,136},{16,144},{24,152},{32,160},{40,168},{48,176},{56,1... | collective-permute-start | bytes 98312 | tf_op jit(solution)/shard_map/ppermute | solution.py:312
  94.5 14.3 %collective-permute-start.7 = (f32[8,1024]{1,0:T(8,128)S(1)}, f32[8,1024]{1,0:T(8,128)S(1)}, u32[]{:S(2)}, u32[]{:S(2)}) collective-permute-start(f32[8,1024]{1,0:T(8,128)S(1)} %get-tuple-element.49), channel_id=1, source_target_pairs={{0,16},{8,24},{16,32},{24,40},{32,48},{40,56},{48,64},{56,72},{64,... | collective-permute-start | bytes 98312 | tf_op jit(solution)/shard_map/ppermute | solution.py:312
  95.8 13.1 %collective-permute-start.11 = (f32[8,1024]{1,0:T(8,128)S(1)}, f32[8,1024]{1,0:T(8,128)S(1)}, u32[]{:S(2)}, u32[]{:S(2)}) collective-permute-start(f32[8,1024]{1,0:T(8,128)S(1)} %get-tuple-element.56), channel_id=1, source_target_pairs={{0,64},{8,72},{16,80},{24,88},{32,96},{40,104},{48,112},{56,120},{... | collective-permute-start | bytes 98312 | tf_op jit(solution)/shard_map/ppermute | solution.py:312
  100.8 8.0 %collective-permute-start.9 = (f32[8,1024]{1,0:T(8,128)S(1)}, f32[8,1024]{1,0:T(8,128)S(1)}, u32[]{:S(2)}, u32[]{:S(2)}) collective-permute-start(f32[8,1024]{1,0:T(8,128)S(1)} %get-tuple-element.52), channel_id=1, source_target_pairs={{0,32},{8,40},{16,48},{24,56},{32,64},{40,72},{48,80},{56,88},{64,... | collective-permute-start | bytes 98312 | tf_op jit(solution)/shard_map/ppermute | solution.py:312
  107.3 2.1 %collective-permute-start.6 = (f32[8,1024]{1,0:T(8,128)S(1)}, f32[8,1024]{1,0:T(8,128)S(1)}, u32[]{:S(2)}, u32[]{:S(2)}) collective-permute-start(f32[8,1024]{1,0:T(8,128)S(1)} %get-tuple-element.48), channel_id=1, source_target_pairs={{0,8},{8,16},{16,24},{24,32},{32,40},{40,48},{48,56},{56,64},{64,7... | collective-permute-start | bytes 98312 | tf_op jit(solution)/shard_map/ppermute | solution.py:312
  139.6 45.0 %copy-start.1 = (bf16[1,8,128,256]{3,2,1,0:T(8,128)(2,1)S(1)}, bf16[1,8,128,256]{3,2,1,0:T(8,128)(2,1)}, u32[]{:S(2)}) copy-start(bf16[1,8,128,256]{3,2,1,0:T(8,128)(2,1)} %param.10) | copy-start | bytes 1572868
  163.7 22.3 %collective-permute-start.16 = (f32[256,384]{1,0:T(8,128)S(1)}, f32[256,384]{1,0:T(8,128)S(1)}, u32[]{:S(2)}, u32[]{:S(2)}) collective-permute-start(f32[256,384]{1,0:T(8,128)S(1)} %bitcast.21), channel_id=1, source_target_pairs={{0,8},{8,0},{1,9},{9,1},{2,10},{10,2},{3,11},{11,3},{4,12},{12,4},... | collective-permute-start | bytes 1179656 | tf_op jit(solution)/shard_map/ppermute | solution.py:367
  165.6 8.7 %collective-permute-start.14 = (bf16[128,256]{1,0:T(8,128)(2,1)S(1)}, bf16[128,256]{1,0:T(8,128)(2,1)S(1)}, u32[]{:S(2)}, u32[]{:S(2)}) collective-permute-start(bf16[128,256]{1,0:T(8,128)(2,1)S(1)} %get-tuple-element.63), channel_id=1, source_target_pairs={{0,1},{1,2},{2,3},{3,4},{4,5},{5,6},{6,7},{8,9},{9,10},{10,11},{11... | collective-permute-start | bytes 196616 | tf_op jit(solution)/shard_map/ppermute | solution.py:312
  172.3 12.2 %collective-permute-start.15 = (bf16[128,256]{1,0:T(8,128)(2,1)S(1)}, bf16[128,256]{1,0:T(8,128)(2,1)S(1)}, u32[]{:S(2)}, u32[]{:S(2)}) collective-permute-start(bf16[128,256]{1,0:T(8,128)(2,1)S(1)} %get-tuple-element.64), channel_id=1, source_target_pairs={{1,0},{2,1},{3,2},{4,3},{5,4},{6,5},{7,6},{9,8},{10,9},{11,10},{12... | collective-permute-start | bytes 196616 | tf_op jit(solution)/shard_map/ppermute | solution.py:312

commit v3 on v2

--- a/solution.py
+++ b/solution.py
@@ -21,6 +21,7 @@
 EXT = CELLS + 2 * COLS
 PAY = 384
 PACK = 64
+RUN = 16
 DISTANCES = (1, 2, 4, 8, 16)
 SLOTS = (4, 1, 0, 2, 3)
 
@@ -54,7 +55,7 @@
 
 def prep_body(
     present, feats_hbm, cot_hbm, w_value_hbm, w_logit_hbm, w_out_hbm, row_hbm, col_hbm, fracs_hbm,
-    values, attn, m16, m2, m1, m8, dattn, accum, gwo, wl_t,
+    values, attn, m16, m2, m1, dattn, accum, gwo, wl_t,
     mix, feats, cot, w_value, w_logit, w_out, row_off, col_off, fracs, sems,
 ):
     frame = lax.axis_index(TM)
@@ -77,10 +78,10 @@
         ((m1, CELLS), (m2, PACK + CELLS)),
         ((m2, 2 * PACK + CELLS),),
         ((m2, 0),),
-        ((m8, CELLS),),
         ((m16, CELLS),),
-    )
-    for message, start in ((m16, 0), (m2, PACK), (m1, 0), (m8, 0)):
+        ((m16, CELLS + PACK),),
+    )
+    for message, start in ((m16, 0), (m2, PACK), (m1, 0)):
         message[pl.ds(start, CELLS), :] = cot[...]
     valid = [None]
     for k in range(K):
@@ -131,6 +132,18 @@
     gwo[...] = mm(mix[...], cot[...], 0, 0)
 
 
+def pick_body(came, own, out):
+    early = lax.rem(lax.axis_index(TM), RUN) < RUN // 2
+
+    @pl.when(early)
+    def _():
+        out[...] = came[pl.ds(0, CELLS + PACK), :]
+
+    @pl.when(jnp.logical_not(early))
+    def _():
+        out[...] = own[pl.ds(0, CELLS + PACK), :]
+
+
 def ext_body(values, low, high, w_value, ext):
     ext[pl.ds(0, COLS), :] = mm(low[...], w_value[...], 1, 0).astype(BF16)
     ext[pl.ds(COLS, CELLS), :] = values[...]
@@ -232,7 +245,7 @@
     return pl.CostEstimate(flops=flops, bytes_accessed=nbytes, transcendentals=0)
 
 
-PARAMS = pltpu.CompilerParams(vmem_limit_bytes=48 * 1024 * 1024)
+PARAMS = pltpu.CompilerParams(vmem_limit_bytes=24 * 1024 * 1024)
 
 
 def prep(present, feats, cot, w_value, w_logit, w_out, row_off, col_off, fracs):
@@ -242,9 +255,8 @@
         out_shape=(
             sds((CELLS, C), BF16),
             sds((H * J, CELLS), F32),
-            sds((CELLS + PACK, C), BF16),
+            sds((CELLS + 2 * PACK, C), BF16),
             sds((CELLS + 3 * PACK, C), BF16),
-            sds((CELLS + PACK, C), BF16),
             sds((CELLS + PACK, C), BF16),
             sds((H, CELLS), F32),
             sds((EXT, C), F32),
@@ -252,7 +264,7 @@
             sds((H * J, C), BF16),
         ),
         in_specs=[SM] + [HB] * 8,
-        out_specs=(VM,) * 10,
+        out_specs=(VM,) * 9,
         scratch_shapes=[
             pltpu.VMEM((CELLS, C), BF16),
             pltpu.VMEM((CELLS, C), BF16),
@@ -318,13 +330,12 @@
     count = size(TM)
     low = shifted(inputs[CELLS - COLS :], "band", 1)
     high = shifted(inputs[:COLS], "band", -1)
-    values, attn, m16, m2, m1, m8, d0, accum, gwo, wl_t = prep(
+    values, attn, m16, m2, m1, d0, accum, gwo, wl_t = prep(
         present, inputs, grad_out, w_value, w_logit.T, w_out, row_offsets[0], col_offsets[0], fractions[0]
     )
     messages = [None] * K
     messages[1] = shifted(m2, TM, -2)
     messages[4] = shifted(m16, TM, -16)
-    messages[3] = shifted(m8, TM, -8)
     near = lax.ppermute(m1, TM, [(i, i - 1) for i in range(1, count, 2)])
     (ext,) = plain(ext_body, (sds((EXT, C), BF16),), [], values, low, high, w_value)
     messages[2] = shifted(messages[1][: CELLS + PACK], TM, -2)
@@ -332,7 +343,14 @@
         messages[1][PACK : CELLS + 2 * PACK], TM, [(i, i + 1) for i in range(0, count, 2)]
     )
     messages[0] = near + far
-    places = ((0, CELLS), (PACK, CELLS + 2 * PACK), (PACK, 0), (0, CELLS), (0, CELLS))
+    if count % RUN == 0:
+        (moved,) = plain(pick_body, (sds((CELLS + PACK, C), BF16),), [], messages[4], m16)
+        messages[3] = lax.ppermute(
+            moved, TM, [(i, i // RUN * RUN + (i + RUN // 2) % RUN) for i in range(count)]
+        )
+    else:
+        messages[3] = shifted(m16[: CELLS + PACK], TM, -8)
+    places = ((0, CELLS), (PACK, CELLS + 2 * PACK), (PACK, 0), (0, CELLS), (0, CELLS + PACK))
     grads = [None] * K
     back = [None] * K
     for k in SLOTS:

time: 188 us -> 200 us (1.064)
  blocking collectives: 52.7 us -> 61.9 us
  waiting for transfers between devices: 41.1 us -> 47.2 us
  starting transfers between devices: 66.1 us -> 62.3 us
    ppermute x13 -> x12, starting transfers between devices: 59.5 us -> 50.1 us  [shifted(): lax.ppermute(value, axis, [(source, source + steps) for source in range(i...]
    all_to_all x1, blocking collectives: 29.2 us -> 35.9 us  [layer(): pieces = lax.all_to_all(pay, both, 0, 0, tiled=True)]
    ppermute x13 -> x12, waiting for transfers between devices: 41.1 us -> 47.2 us  [shifted(): lax.ppermute(value, axis, [(source, source + steps) for source in range(i...]
    ppermute x0 -> x1, starting transfers between devices: none -> 5.75 us  [layer(): lax.ppermute(moved, TM, [(i, i // RUN * RUN + (i + RUN // 2) % RUN) for i...]
    all_to_all x1, blocking collectives: 23.6 us -> 26 us  [layer(): own = lax.all_to_all(spread, both, 0, 0, tiled=True)]
where the time goes in v3:
time: 200 us; the launch traced here: 199 us
  starting transfers between devices  62.3 us (31%)
  blocking collectives  61.9 us (31%)
  waiting for transfers between devices  47.2 us (24%)
  Pallas kernels  23.1 us (12%)
  local copies, waits for them, and re-layouts  2.12 us (1%)
    ppermute x12, starting transfers between devices, shifted(): lax.ppermute(value, axis, [(source, source + steps) for source in range(i...  50.1 us
    ppermute x12, waiting for transfers between devices, shifted(): lax.ppermute(value, axis, [(source, source + steps) for source in range(i...  47.2 us
    all_to_all x1, blocking collectives, layer(): pieces = lax.all_to_all(pay, both, 0, 0, tiled=True)  35.9 us
    all_to_all x1, blocking collectives, layer(): own = lax.all_to_all(spread, both, 0, 0, tiled=True)  26 us
    pallas_call x5, Pallas kernels, slot_call(): pl.pallas_call(functools.partial(slot_body, cot_at, pack_at), name='slot'...  15.1 us
    ppermute x1, starting transfers between devices, layer(): lax.ppermute(moved, TM, [(i, i // RUN * RUN + (i + RUN // 2) % RUN) for i...  5.75 us
    pallas_call x1, Pallas kernels, prep(): pl.pallas_call(prep_body, name='prep', out_shape=(sds((CELLS, C), BF16),...  5.38 us
  transfers between devices with their start and end apart: 17, of which 7 were waited for; matrix products, arithmetic and copies ran while one was open for 0% of the time, Pallas kernels for 7%

profile of v3, /device:TPU:6, one launch (start us, length us, event | category | flops | bytes accessed | tf_op | source)
XLA Modules:
  0.0 199.0 jit_solution(15579863037047680115)
XLA Ops:
  1.3 5.4 %prep.1 = (bf16[1024,256]{1,0:T(8,128)(2,1)S(1)}, f32[48,1024]{1,0:T(8,128)S(1)}, bf16[1152,256]{1,0:T(8,128)(2,1)S(1)}, bf16[1216,256]{1,0:T(8,128)(2,1)S(1)}, ...) custom-call(s32[1,5]{1,0:T(1,128)S(1)} %copy-done.4, ...), custom_call_target="tpu_custom_call" | custom-call | flops 1000000000 | bytes 4000000 | tf_op jit(solution)/shard_map/prep/pallas_call | solution.py:252
  6.7 1.3 collective-permute-start.1
  8.0 1.3 collective-permute-start.5
  9.3 1.3 collective-permute-start
  10.6 17.9 %collective-permute-done.5.message.came = bf16[1152,256]{1,0:T(8,128)(2,1)S(1)} collective-permute-done((bf16[1152,256]{1,0:T(8,128)(2,1)S(1)}, bf16[1152,256]{1,0:T(8,128)(2,1)S(1)}, u32[]{:S(2)}, u32[]{:S(2)}) %collective-permute-start.5) | collective-permute-done | bytes 589856 | tf_op jit(solution)/shard_map/ppermute | solution.py:324
  28.5 5.7 %collective-permute-start.10 = (bf16[1088,256]{1,0:T(8,128)(2,1)S(1)}, bf16[1088,256]{1,0:T(8,128)(2,1)S(1)}, u32[]{:S(2)}, u32[]{:S(2)}) collective-permute-start(bf16[1088,256]{1,0:T(8,128)(2,1)S(1)} %shard_map.121), channel_id=1, source_target_pairs={{0,64},{8,72},{16,80},{24,88},{32,96},{40,104},{48,112},{56,120},{... | collective-permute-start | bytes 1671176 | tf_op jit(solution)/shard_map/ppermute | solution.py:348
  34.4 1.4 collective-permute-start.8
  35.8 1.3 collective-permute-start.2
  37.2 2.7 %collective-permute-start.4 = (bf16[128,256]{1,0:T(8,128)(2,1)S(1)}, bf16[128,256]{1,0:T(8,128)(2,1)S(1)}, u32[]{:S(2)}, u32[]{:S(2)}) collective-permute-start(bf16[128,256]{1,0:T(8,128)(2,1)S(1)} %get-tuple-element.76), channel_id=1, source_target_pairs={{1,0},{2,1},{3,2},{4,3},{5,4},{6,5},{7,6},{9,8},{10,9},{11,10},{12... | collective-permute-start | bytes 196616 | tf_op jit(solution)/shard_map/ppermute | solution.py:324
  39.9 9.7 %collective-permute-done.4.high = bf16[128,256]{1,0:T(8,128)(2,1)S(1)} collective-permute-done((bf16[128,256]{1,0:T(8,128)(2,1)S(1)}, bf16[128,256]{1,0:T(8,128)(2,1)S(1)}, u32[]{:S(2)}, u32[]{:S(2)}) %collective-permute-start.4) | collective-permute-done | bytes 65568 | tf_op jit(solution)/shard_map/ppermute | solution.py:324
  49.6 4.1 %collective-permute-start.3 = (bf16[128,256]{1,0:T(8,128)(2,1)S(1)}, bf16[128,256]{1,0:T(8,128)(2,1)S(1)}, u32[]{:S(2)}, u32[]{:S(2)}) collective-permute-start(bf16[128,256]{1,0:T(8,128)(2,1)S(1)} %get-tuple-element.77), channel_id=1, source_target_pairs={{0,1},{1,2},{2,3},{3,4},{4,5},{5,6},{6,7},{8,9},{9,10},{10,11},{11... | collective-permute-start | bytes 196616 | tf_op jit(solution)/shard_map/ppermute | solution.py:324
  53.7 2.0 %collective-permute-done.3.low = bf16[128,256]{1,0:T(8,128)(2,1)S(1)} collective-permute-done((bf16[128,256]{1,0:T(8,128)(2,1)S(1)}, bf16[128,256]{1,0:T(8,128)(2,1)S(1)}, u32[]{:S(2)}, u32[]{:S(2)}) %collective-permute-start.3) | collective-permute-done | bytes 65568 | tf_op jit(solution)/shard_map/ppermute | solution.py:324
  56.0 3.0 %slot.5 = (f32[8,1024]{1,0:T(8,128)S(1)}, f32[1280,256]{1,0:T(8,128)S(1)}, f32[256,256]{1,0:T(8,128)S(1)}) custom-call(bf16[1152,256]{1,0:T(8,128)(2,1)S(1)} %collective-permute-done.5.message.came, bf16[1280,256]{1,0:T(8,128)(2,1)S(1)} %shard_map.120.ext, bf16[256,256]{1,0:T(8,128)(2,1)S(1)} %copy-done.3, ...), custom_call_target="tpu_custom_call", output_to_operand_aliasing={{1}: (3, {}), {2}: (4, {})} | custom-call | flops 1000000000 | bytes 4000000 | tf_op jit(solution)/shard_map/slot/pallas_call | solution.py:292
  59.0 3.0 %slot.6 = (f32[8,1024]{1,0:T(8,128)S(1)}, f32[1280,256]{1,0:T(8,128)S(1)}, f32[256,256]{1,0:T(8,128)S(1)}) custom-call(bf16[1216,256]{1,0:T(8,128)(2,1)S(1)} %collective-permute-done.1.message, bf16[1280,256]{1,0:T(8,128)(2,1)S(1)} %shard_map.120.ext, bf16[256,256]{1,0:T(8,128)(2,1)S(1)} %copy-done.3, ...), custom_call_target="tpu_custom_call", output_to_operand_aliasing={{1}: (3, {}), {2}: (4, {})} | custom-call | flops 1000000000 | bytes 4000000 | tf_op jit(solution)/shard_map/slot/pallas_call | solution.py:292
  62.2 3.0 %slot.7 = (f32[8,1024]{1,0:T(8,128)S(1)}, f32[1280,256]{1,0:T(8,128)S(1)}, f32[256,256]{1,0:T(8,128)S(1)}) custom-call(bf16[1088,256]{1,0:T(8,128)(2,1)S(1)} %add.6.message, bf16[1280,256]{1,0:T(8,128)(2,1)S(1)} %shard_map.120.ext, bf16[256,256]{1,0:T(8,128)(2,1)S(1)} %copy-done.3, ...), custom_call_target="tpu_custom_call", output_to_operand_aliasing={{1}: (3, {}), {2}: (4, {})} | custom-call | flops 1000000000 | bytes 4000000 | tf_op jit(solution)/shard_map/slot/pallas_call | solution.py:292
  65.3 6.0 %collective-permute-done.8.message = bf16[1088,256]{1,0:T(8,128)(2,1)S(1)} collective-permute-done((bf16[1088,256]{1,0:T(8,128)(2,1)S(1)}, bf16[1088,256]{1,0:T(8,128)(2,1)S(1)}, u32[]{:S(2)}, u32[]{:S(2)}) %collective-permute-start.8) | collective-permute-done | bytes 557088 | tf_op jit(solution)/shard_map/ppermute | solution.py:324
  71.2 3.0 %slot.8 = (f32[8,1024]{1,0:T(8,128)S(1)}, f32[1280,256]{1,0:T(8,128)S(1)}, f32[256,256]{1,0:T(8,128)S(1)}) custom-call(bf16[1088,256]{1,0:T(8,128)(2,1)S(1)} %collective-permute-done.8.message, bf16[1280,256]{1,0:T(8,128)(2,1)S(1)} %shard_map.120.ext, bf16[256,256]{1,0:T(8,128)(2,1)S(1)} %copy-done.3, ...), custom_call_target="tpu_custom_call", output_to_operand_aliasing={{1}: (3, {}), {2}: (4, {})} | custom-call | flops 1000000000 | bytes 4000000 | tf_op jit(solution)/shard_map/slot/pallas_call | solution.py:292
  74.3 3.0 %slot.9 = (f32[8,1024]{1,0:T(8,128)S(1)}, f32[1280,256]{1,0:T(8,128)S(1)}, f32[256,256]{1,0:T(8,128)S(1)}) custom-call(bf16[1088,256]{1,0:T(8,128)(2,1)S(1)} %collective-permute-done.10.message, bf16[1280,256]{1,0:T(8,128)(2,1)S(1)} %shard_map.120.ext, bf16[256,256]{1,0:T(8,128)(2,1)S(1)} %copy-done.3, ...), custom_call_target="tpu_custom_call", output_to_operand_aliasing={{1}: (3, {}), {2}: (4, {})} | custom-call | flops 1000000000 | bytes 4000000 | tf_op jit(solution)/shard_map/slot/pallas_call | solution.py:292
  77.7 1.9 collective-permute-start.13
  79.7 9.4 %collective-permute-start.12 = (f32[8,1024]{1,0:T(8,128)S(1)}, f32[8,1024]{1,0:T(8,128)S(1)}, u32[]{:S(2)}, u32[]{:S(2)}) collective-permute-start(f32[8,1024]{1,0:T(8,128)S(1)} %get-tuple-element.55), channel_id=1, source_target_pairs={{0,128},{8,136},{16,144},{24,152},{32,160},{40,168},{48,176},{56,1... | collective-permute-start | bytes 98312 | tf_op jit(solution)/shard_map/ppermute | solution.py:324
  89.1 1.3 collective-permute-start.7
  90.4 2.1 %collective-permute-start.6 = (f32[8,1024]{1,0:T(8,128)S(1)}, f32[8,1024]{1,0:T(8,128)S(1)}, u32[]{:S(2)}, u32[]{:S(2)}) collective-permute-start(f32[8,1024]{1,0:T(8,128)S(1)} %get-tuple-element.47), channel_id=1, source_target_pairs={{0,8},{8,16},{16,24},{24,32},{32,40},{40,48},{48,56},{56,64},{64,7... | collective-permute-start | bytes 98312 | tf_op jit(solution)/shard_map/ppermute | solution.py:324
  92.5 6.3 %collective-permute-start.9 = (f32[8,1024]{1,0:T(8,128)S(1)}, f32[8,1024]{1,0:T(8,128)S(1)}, u32[]{:S(2)}, u32[]{:S(2)}) collective-permute-start(f32[8,1024]{1,0:T(8,128)S(1)} %get-tuple-element.51), channel_id=1, source_target_pairs={{0,32},{8,40},{16,48},{24,56},{32,64},{40,72},{48,80},{56,88},{64,... | collective-permute-start | bytes 98312 | tf_op jit(solution)/shard_map/ppermute | solution.py:324
  98.8 11.6 %collective-permute-start.11 = (f32[8,1024]{1,0:T(8,128)S(1)}, f32[8,1024]{1,0:T(8,128)S(1)}, u32[]{:S(2)}, u32[]{:S(2)}) collective-permute-start(f32[8,1024]{1,0:T(8,128)S(1)} %get-tuple-element.54), channel_id=1, source_target_pairs={{0,64},{8,72},{16,80},{24,88},{32,96},{40,104},{48,112},{56,120},{... | collective-permute-start | bytes 98312 | tf_op jit(solution)/shard_map/ppermute | solution.py:324
  110.4 1.3 collective-permute-done.11.d4
  112.7 35.9 %all_to_all.18 = f32[256,1,384]{2,1,0:T(1,128)S(1)} all-to-all(f32[256,1,384]{2,1,0:T(1,128)S(1)} %copy.24), channel_id=1, replica_groups=mesh['pair'=32,'core'=2,'band'=8] {'pair','band'}, dimensions={0} | all-to-all | bytes 786432 | tf_op jit(solution)/shard_map/all_to_all | solution.py:375
  149.1 26.0 %all_to_all.19 = f32[256,1,384]{2,1,0:T(1,128)S(1)} all-to-all(f32[256,1,384]{2,1,0:T(1,128)S(1)} %reshape.38), channel_id=1, replica_groups=mesh['pair'=32,'core'=2,'band'=8] {'pair','band'}, dimensions={0} | all-to-all | bytes 786432 | tf_op jit(solution)/shard_map/all_to_all | solution.py:380
  175.2 1.9 collective-permute-start.16
  177.1 6.7 %collective-permute-start.14 = (bf16[128,256]{1,0:T(8,128)(2,1)S(1)}, bf16[128,256]{1,0:T(8,128)(2,1)S(1)}, u32[]{:S(2)}, u32[]{:S(2)}) collective-permute-start(bf16[128,256]{1,0:T(8,128)(2,1)S(1)} %get-tuple-element.61), channel_id=1, source_target_pairs={{0,1},{1,2},{2,3},{3,4},{4,5},{5,6},{6,7},{8,9},{9,10},{10,11},{11... | collective-permute-start | bytes 196616 | tf_op jit(solution)/shard_map/ppermute | solution.py:324
  183.8 1.9 collective-permute-start.15
  185.8 10.2 %collective-permute-done.15.from_next = bf16[128,256]{1,0:T(8,128)(2,1)S(1)} collective-permute-done((bf16[128,256]{1,0:T(8,128)(2,1)S(1)}, bf16[128,256]{1,0:T(8,128)(2,1)S(1)}, u32[]{:S(2)}, u32[]{:S(2)}) %collective-permute-start.15) | collective-permute-done | bytes 65568 | tf_op jit(solution)/shard_map/ppermute | solution.py:324
  196.0 1.4 shard_map.124
  (37 shorter events, 4.7 us)
Async XLA Ops:
  0.6 0.7 copy-start.4
  6.7 27.6 %collective-permute-start.1 = (bf16[1216,256]{1,0:T(8,128)(2,1)S(1)}, bf16[1216,256]{1,0:T(8,128)(2,1)S(1)}, u32[]{:S(2)}, u32[]{:S(2)}) collective-permute-start(bf16[1216,256]{1,0:T(8,128)(2,1)S(1)} %get-tuple-element.38), channel_id=1, source_target_pairs={{16,0},{24,8},{32,16},{40,24},{48,32},{56,40},{64,48},{72,56},{80,... | collective-permute-start | bytes 1867784 | tf_op jit(solution)/shard_map/ppermute | solution.py:324
  8.0 20.5 %collective-permute-start.5 = (bf16[1152,256]{1,0:T(8,128)(2,1)S(1)}, bf16[1152,256]{1,0:T(8,128)(2,1)S(1)}, u32[]{:S(2)}, u32[]{:S(2)}) collective-permute-start(bf16[1152,256]{1,0:T(8,128)(2,1)S(1)} %get-tuple-element.40.own), channel_id=1, source_target_pairs={{128,0},{136,8},{144,16},{152,24},{160,32},{168,40},{176,48},{184,... | collective-permute-start | bytes 1769480 | tf_op jit(solution)/shard_map/ppermute | solution.py:324
  9.3 52.8 %collective-permute-start = (bf16[1088,256]{1,0:T(8,128)(2,1)S(1)}, bf16[1088,256]{1,0:T(8,128)(2,1)S(1)}, u32[]{:S(2)}, u32[]{:S(2)}) collective-permute-start(bf16[1088,256]{1,0:T(8,128)(2,1)S(1)} %get-tuple-element.37), channel_id=1, source_target_pairs={{8,0},{24,16},{40,32},{56,48},{72,64},{88,80},{104,96},{120,112},{... | collective-permute-start | bytes 1671176 | tf_op jit(solution)/shard_map/ppermute | solution.py:339
  28.5 8.7 %copy-start = (bf16[1,8,128,256]{3,2,1,0:T(8,128)(2,1)S(1)}, bf16[1,8,128,256]{3,2,1,0:T(8,128)(2,1)}, u32[]{:S(2)}) copy-start(bf16[1,8,128,256]{3,2,1,0:T(8,128)(2,1)} %param.9) | copy-start | bytes 1572868
  28.5 27.2 %copy-start.2 = (bf16[256,256]{1,0:T(8,128)(2,1)S(1)}, bf16[256,256]{1,0:T(8,128)(2,1)}, u32[]{:S(2)}) copy-start(bf16[256,256]{1,0:T(8,128)(2,1)} %w_value.3) | copy-start | bytes 393220
  28.5 45.7 %collective-permute-start.10 = (bf16[1088,256]{1,0:T(8,128)(2,1)S(1)}, bf16[1088,256]{1,0:T(8,128)(2,1)S(1)}, u32[]{:S(2)}, u32[]{:S(2)}) collective-permute-start(bf16[1088,256]{1,0:T(8,128)(2,1)S(1)} %shard_map.121), channel_id=1, source_target_pairs={{0,64},{8,72},{16,80},{24,88},{32,96},{40,104},{48,112},{56,120},{... | collective-permute-start | bytes 1671176 | tf_op jit(solution)/shard_map/ppermute | solution.py:348
  34.4 21.6 %copy-start.3 = (bf16[256,256]{1,0:T(8,128)(2,1)S(1)}, bf16[256,256]{1,0:T(8,128)(2,1)}, u32[]{:S(2)}) copy-start(bf16[256,256]{1,0:T(8,128)(2,1)} %w_out.9) | copy-start | bytes 393220
  34.4 36.8 %collective-permute-start.8 = (bf16[1088,256]{1,0:T(8,128)(2,1)S(1)}, bf16[1088,256]{1,0:T(8,128)(2,1)S(1)}, u32[]{:S(2)}, u32[]{:S(2)}) collective-permute-start(bf16[1088,256]{1,0:T(8,128)(2,1)S(1)} %get-tuple-element.74), channel_id=1, source_target_pairs={{16,0},{24,8},{32,16},{40,24},{48,32},{56,40},{64,48},{72,56},{80,... | collective-permute-start | bytes 1671176 | tf_op jit(solution)/shard_map/ppermute | solution.py:324
  35.8 26.2 %collective-permute-start.2 = (bf16[1088,256]{1,0:T(8,128)(2,1)S(1)}, bf16[1088,256]{1,0:T(8,128)(2,1)S(1)}, u32[]{:S(2)}, u32[]{:S(2)}) collective-permute-start(bf16[1088,256]{1,0:T(8,128)(2,1)S(1)} %get-tuple-element.75), channel_id=1, source_target_pairs={{0,8},{16,24},{32,40},{48,56},{64,72},{80,88},{96,104},{112,120},{... | collective-permute-start | bytes 1671176 | tf_op jit(solution)/shard_map/ppermute | solution.py:342
  37.2 12.4 %collective-permute-start.4 = (bf16[128,256]{1,0:T(8,128)(2,1)S(1)}, bf16[128,256]{1,0:T(8,128)(2,1)S(1)}, u32[]{:S(2)}, u32[]{:S(2)}) collective-permute-start(bf16[128,256]{1,0:T(8,128)(2,1)S(1)} %get-tuple-element.76), channel_id=1, source_target_pairs={{1,0},{2,1},{3,2},{4,3},{5,4},{6,5},{7,6},{9,8},{10,9},{11,10},{12... | collective-permute-start | bytes 196616 | tf_op jit(solution)/shard_map/ppermute | solution.py:324
  49.6 6.1 %collective-permute-start.3 = (bf16[128,256]{1,0:T(8,128)(2,1)S(1)}, bf16[128,256]{1,0:T(8,128)(2,1)S(1)}, u32[]{:S(2)}, u32[]{:S(2)}) collective-permute-start(bf16[128,256]{1,0:T(8,128)(2,1)S(1)} %get-tuple-element.77), channel_id=1, source_target_pairs={{0,1},{1,2},{2,3},{3,4},{4,5},{5,6},{6,7},{8,9},{9,10},{10,11},{11... | collective-permute-start | bytes 196616 | tf_op jit(solution)/shard_map/ppermute | solution.py:324
  77.7 34.0 %collective-permute-start.13 = (f32[256,256]{1,0:T(8,128)S(1)}, f32[256,256]{1,0:T(8,128)S(1)}, u32[]{:S(2)}, u32[]{:S(2)}) collective-permute-start(f32[256,256]{1,0:T(8,128)S(1)} %get-tuple-element.59), channel_id=1, source_target_pairs={{0,8},{8,0},{1,9},{9,1},{2,10},{10,2},{3,11},{11,3},{4,12},{12,4},... | collective-permute-start | bytes 786440 | tf_op jit(solution)/shard_map/ppermute | solution.py:366
  79.7 19.1 %collective-permute-start.12 = (f32[8,1024]{1,0:T(8,128)S(1)}, f32[8,1024]{1,0:T(8,128)S(1)}, u32[]{:S(2)}, u32[]{:S(2)}) collective-permute-start(f32[8,1024]{1,0:T(8,128)S(1)} %get-tuple-element.55), channel_id=1, source_target_pairs={{0,128},{8,136},{16,144},{24,152},{32,160},{40,168},{48,176},{56,1... | collective-permute-start | bytes 98312 | tf_op jit(solution)/shard_map/ppermute | solution.py:324
  89.1 21.3 %collective-permute-start.7 = (f32[8,1024]{1,0:T(8,128)S(1)}, f32[8,1024]{1,0:T(8,128)S(1)}, u32[]{:S(2)}, u32[]{:S(2)}) collective-permute-start(f32[8,1024]{1,0:T(8,128)S(1)} %get-tuple-element.48), channel_id=1, source_target_pairs={{0,16},{8,24},{16,32},{24,40},{32,48},{40,56},{48,64},{56,72},{64,... | collective-permute-start | bytes 98312 | tf_op jit(solution)/shard_map/ppermute | solution.py:324
  90.4 20.0 %collective-permute-start.6 = (f32[8,1024]{1,0:T(8,128)S(1)}, f32[8,1024]{1,0:T(8,128)S(1)}, u32[]{:S(2)}, u32[]{:S(2)}) collective-permute-start(f32[8,1024]{1,0:T(8,128)S(1)} %get-tuple-element.47), channel_id=1, source_target_pairs={{0,8},{8,16},{16,24},{24,32},{32,40},{40,48},{48,56},{56,64},{64,7... | collective-permute-start | bytes 98312 | tf_op jit(solution)/shard_map/ppermute | solution.py:324
  92.5 17.9 %collective-permute-start.9 = (f32[8,1024]{1,0:T(8,128)S(1)}, f32[8,1024]{1,0:T(8,128)S(1)}, u32[]{:S(2)}, u32[]{:S(2)}) collective-permute-start(f32[8,1024]{1,0:T(8,128)S(1)} %get-tuple-element.51), channel_id=1, source_target_pairs={{0,32},{8,40},{16,48},{24,56},{32,64},{40,72},{48,80},{56,88},{64,... | collective-permute-start | bytes 98312 | tf_op jit(solution)/shard_map/ppermute | solution.py:324
  98.8 12.9 %collective-permute-start.11 = (f32[8,1024]{1,0:T(8,128)S(1)}, f32[8,1024]{1,0:T(8,128)S(1)}, u32[]{:S(2)}, u32[]{:S(2)}) collective-permute-start(f32[8,1024]{1,0:T(8,128)S(1)} %get-tuple-element.54), channel_id=1, source_target_pairs={{0,64},{8,72},{16,80},{24,88},{32,96},{40,104},{48,112},{56,120},{... | collective-permute-start | bytes 98312 | tf_op jit(solution)/shard_map/ppermute | solution.py:324
  148.6 47.4 %copy-start.1 = (bf16[1,8,128,256]{3,2,1,0:T(8,128)(2,1)S(1)}, bf16[1,8,128,256]{3,2,1,0:T(8,128)(2,1)}, u32[]{:S(2)}) copy-start(bf16[1,8,128,256]{3,2,1,0:T(8,128)(2,1)} %param.10) | copy-start | bytes 1572868
  175.2 22.3 %collective-permute-start.16 = (f32[256,384]{1,0:T(8,128)S(1)}, f32[256,384]{1,0:T(8,128)S(1)}, u32[]{:S(2)}, u32[]{:S(2)}) collective-permute-start(f32[256,384]{1,0:T(8,128)S(1)} %bitcast.21), channel_id=1, source_target_pairs={{0,8},{8,0},{1,9},{9,1},{2,10},{10,2},{3,11},{11,3},{4,12},{12,4},... | collective-permute-start | bytes 1179656 | tf_op jit(solution)/shard_map/ppermute | solution.py:385
  177.1 8.7 %collective-permute-start.14 = (bf16[128,256]{1,0:T(8,128)(2,1)S(1)}, bf16[128,256]{1,0:T(8,128)(2,1)S(1)}, u32[]{:S(2)}, u32[]{:S(2)}) collective-permute-start(bf16[128,256]{1,0:T(8,128)(2,1)S(1)} %get-tuple-element.61), channel_id=1, source_target_pairs={{0,1},{1,2},{2,3},{3,4},{4,5},{5,6},{6,7},{8,9},{9,10},{10,11},{11... | collective-permute-start | bytes 196616 | tf_op jit(solution)/shard_map/ppermute | solution.py:324
  183.8 12.2 %collective-permute-start.15 = (bf16[128,256]{1,0:T(8,128)(2,1)S(1)}, bf16[128,256]{1,0:T(8,128)(2,1)S(1)}, u32[]{:S(2)}, u32[]{:S(2)}) collective-permute-start(bf16[128,256]{1,0:T(8,128)(2,1)S(1)} %get-tuple-element.62), channel_id=1, source_target_pairs={{1,0},{2,1},{3,2},{4,3},{5,4},{6,5},{7,6},{9,8},{10,9},{11,10},{12... | collective-permute-start | bytes 196616 | tf_op jit(solution)/shard_map/ppermute | solution.py:324

commit v4 on v3

--- a/solution.py
+++ b/solution.py
@@ -21,9 +21,8 @@
 EXT = CELLS + 2 * COLS
 PAY = 384
 PACK = 64
-RUN = 16
 DISTANCES = (1, 2, 4, 8, 16)
-SLOTS = (4, 1, 0, 2, 3)
+SLOTS = (1, 0, 4, 2, 3)
 
 TM = ("pair", "core")
 
@@ -132,18 +131,6 @@
     gwo[...] = mm(mix[...], cot[...], 0, 0)
 
 
-def pick_body(came, own, out):
-    early = lax.rem(lax.axis_index(TM), RUN) < RUN // 2
-
-    @pl.when(early)
-    def _():
-        out[...] = came[pl.ds(0, CELLS + PACK), :]
-
-    @pl.when(jnp.logical_not(early))
-    def _():
-        out[...] = own[pl.ds(0, CELLS + PACK), :]
-
-
 def ext_body(values, low, high, w_value, ext):
     ext[pl.ds(0, COLS), :] = mm(low[...], w_value[...], 1, 0).astype(BF16)
     ext[pl.ds(COLS, CELLS), :] = values[...]
@@ -343,13 +330,7 @@
         messages[1][PACK : CELLS + 2 * PACK], TM, [(i, i + 1) for i in range(0, count, 2)]
     )
     messages[0] = near + far
-    if count % RUN == 0:
-        (moved,) = plain(pick_body, (sds((CELLS + PACK, C), BF16),), [], messages[4], m16)
-        messages[3] = lax.ppermute(
-            moved, TM, [(i, i // RUN * RUN + (i + RUN // 2) % RUN) for i in range(count)]
-        )
-    else:
-        messages[3] = shifted(m16[: CELLS + PACK], TM, -8)
+    messages[3] = shifted(m16[: CELLS + PACK], TM, -8)
     places = ((0, CELLS), (PACK, CELLS + 2 * PACK), (PACK, 0), (0, CELLS), (0, CELLS + PACK))
     grads = [None] * K
     back = [None] * K

time: 200 us -> 188 us (0.940)
  blocking collectives: 61.9 us -> 52.8 us
  waiting for transfers between devices: 47.2 us -> 40.9 us
  starting transfers between devices: 62.3 us -> 66.2 us
    ppermute x12 -> x13, starting transfers between devices: 50.1 us -> 59.8 us  [shifted(): lax.ppermute(value, axis, [(source, source + steps) for source in range(i...]
    all_to_all x1, blocking collectives: 35.9 us -> 29.2 us  [layer(): pieces = lax.all_to_all(pay, both, 0, 0, tiled=True)]
    ppermute x12 -> x13, waiting for transfers between devices: 47.2 us -> 40.9 us  [shifted(): lax.ppermute(value, axis, [(source, source + steps) for source in range(i...]
    ppermute x1 -> x0, starting transfers between devices: 5.75 us -> none  [layer(): lax.ppermute(moved, TM, [(i, i // RUN * RUN + (i + RUN // 2) % RUN) for i...]
    all_to_all x1, blocking collectives: 26 us -> 23.6 us  [layer(): own = lax.all_to_all(spread, both, 0, 0, tiled=True)]
where the time goes in v4:
time: 188 us
  starting transfers between devices  66.2 us (35%)
  blocking collectives  52.8 us (28%)
  waiting for transfers between devices  40.9 us (22%)
  Pallas kernels  23.1 us (12%)
  local copies, waits for them, and re-layouts  2.15 us (1%)
    ppermute x13, starting transfers between devices, shifted(): lax.ppermute(value, axis, [(source, source + steps) for source in range(i...  59.8 us
    ppermute x13, waiting for transfers between devices, shifted(): lax.ppermute(value, axis, [(source, source + steps) for source in range(i...  40.9 us
    all_to_all x1, blocking collectives, layer(): pieces = lax.all_to_all(pay, both, 0, 0, tiled=True)  29.2 us
    all_to_all x1, blocking collectives, layer(): own = lax.all_to_all(spread, both, 0, 0, tiled=True)  23.6 us
    pallas_call x5, Pallas kernels, slot_call(): pl.pallas_call(functools.partial(slot_body, cot_at, pack_at), name='slot'...  15.1 us
    pallas_call x1, Pallas kernels, prep(): pl.pallas_call(prep_body, name='prep', out_shape=(sds((CELLS, C), BF16),...  5.38 us
  transfers between devices with their start and end apart: 17, of which 7 were waited for; matrix products, arithmetic and copies ran while one was open for 0% of the time, Pallas kernels for 7%

profile of v4, /device:TPU:6, one launch (start us, length us, event | category | flops | bytes accessed | tf_op | source)
XLA Modules:
  0.0 187.5 jit_solution(821451357796290185)
XLA Ops:
  1.3 5.4 %prep.1 = (bf16[1024,256]{1,0:T(8,128)(2,1)S(1)}, f32[48,1024]{1,0:T(8,128)S(1)}, bf16[1152,256]{1,0:T(8,128)(2,1)S(1)}, bf16[1216,256]{1,0:T(8,128)(2,1)S(1)}, ...) custom-call(s32[1,5]{1,0:T(1,128)S(1)} %copy-done.4, ...), custom_call_target="tpu_custom_call" | custom-call | flops 1000000000 | bytes 4000000 | tf_op jit(solution)/shard_map/prep/pallas_call | solution.py:239
  6.7 1.4 collective-permute-start.1
  8.1 1.3 collective-permute-start
  9.4 1.4 collective-permute-start.8
  10.9 13.6 %collective-permute-done.1.message = bf16[1216,256]{1,0:T(8,128)(2,1)S(1)} collective-permute-done((bf16[1216,256]{1,0:T(8,128)(2,1)S(1)}, bf16[1216,256]{1,0:T(8,128)(2,1)S(1)}, u32[]{:S(2)}, u32[]{:S(2)}) %collective-permute-start.1) | collective-permute-done | bytes 622624 | tf_op jit(solution)/shard_map/ppermute | solution.py:311
  24.6 1.3 collective-permute-start.2
  25.9 11.0 %collective-permute-start.3 = (bf16[128,256]{1,0:T(8,128)(2,1)S(1)}, bf16[128,256]{1,0:T(8,128)(2,1)S(1)}, u32[]{:S(2)}, u32[]{:S(2)}) collective-permute-start(bf16[128,256]{1,0:T(8,128)(2,1)S(1)} %get-tuple-element.77), channel_id=1, source_target_pairs={{0,1},{1,2},{2,3},{3,4},{4,5},{5,6},{6,7},{8,9},{9,10},{10,11},{11... | collective-permute-start | bytes 196616 | tf_op jit(solution)/shard_map/ppermute | solution.py:311
  36.9 1.3 collective-permute-start.7
  38.8 1.9 %collective-permute-start.4 = (bf16[128,256]{1,0:T(8,128)(2,1)S(1)}, bf16[128,256]{1,0:T(8,128)(2,1)S(1)}, u32[]{:S(2)}, u32[]{:S(2)}) collective-permute-start(bf16[128,256]{1,0:T(8,128)(2,1)S(1)} %get-tuple-element.76), channel_id=1, source_target_pairs={{1,0},{2,1},{3,2},{4,3},{5,4},{6,5},{7,6},{9,8},{10,9},{11,10},{12... | collective-permute-start | bytes 196616 | tf_op jit(solution)/shard_map/ppermute | solution.py:311
  40.8 10.5 %collective-permute-done.4.high = bf16[128,256]{1,0:T(8,128)(2,1)S(1)} collective-permute-done((bf16[128,256]{1,0:T(8,128)(2,1)S(1)}, bf16[128,256]{1,0:T(8,128)(2,1)S(1)}, u32[]{:S(2)}, u32[]{:S(2)}) %collective-permute-start.4) | collective-permute-done | bytes 65568 | tf_op jit(solution)/shard_map/ppermute | solution.py:311
  51.3 1.5 collective-permute-start.10
  53.0 3.0 %slot.5 = (f32[8,1024]{1,0:T(8,128)S(1)}, f32[1280,256]{1,0:T(8,128)S(1)}, f32[256,256]{1,0:T(8,128)S(1)}) custom-call(bf16[1216,256]{1,0:T(8,128)(2,1)S(1)} %collective-permute-done.1.message, bf16[1280,256]{1,0:T(8,128)(2,1)S(1)} %shard_map.120.ext, bf16[256,256]{1,0:T(8,128)(2,1)S(1)} %copy-done.3, ...), custom_call_target="tpu_custom_call", output_to_operand_aliasing={{1}: (3, {}), {2}: (4, {})} | custom-call | flops 1000000000 | bytes 4000000 | tf_op jit(solution)/shard_map/slot/pallas_call | solution.py:279
  56.2 3.0 %slot.6 = (f32[8,1024]{1,0:T(8,128)S(1)}, f32[1280,256]{1,0:T(8,128)S(1)}, f32[256,256]{1,0:T(8,128)S(1)}) custom-call(bf16[1088,256]{1,0:T(8,128)(2,1)S(1)} %add.6.message, bf16[1280,256]{1,0:T(8,128)(2,1)S(1)} %shard_map.120.ext, bf16[256,256]{1,0:T(8,128)(2,1)S(1)} %copy-done.3, ...), custom_call_target="tpu_custom_call", output_to_operand_aliasing={{1}: (3, {}), {2}: (4, {})} | custom-call | flops 1000000000 | bytes 4000000 | tf_op jit(solution)/shard_map/slot/pallas_call | solution.py:279
  59.2 3.0 %slot.7 = (f32[8,1024]{1,0:T(8,128)S(1)}, f32[1280,256]{1,0:T(8,128)S(1)}, f32[256,256]{1,0:T(8,128)S(1)}) custom-call(bf16[1152,256]{1,0:T(8,128)(2,1)S(1)} %collective-permute-done.8.message, bf16[1280,256]{1,0:T(8,128)(2,1)S(1)} %shard_map.120.ext, bf16[256,256]{1,0:T(8,128)(2,1)S(1)} %copy-done.3, ...), custom_call_target="tpu_custom_call", output_to_operand_aliasing={{1}: (3, {}), {2}: (4, {})} | custom-call | flops 1000000000 | bytes 4000000 | tf_op jit(solution)/shard_map/slot/pallas_call | solution.py:279
  62.3 3.0 %slot.8 = (f32[8,1024]{1,0:T(8,128)S(1)}, f32[1280,256]{1,0:T(8,128)S(1)}, f32[256,256]{1,0:T(8,128)S(1)}) custom-call(bf16[1088,256]{1,0:T(8,128)(2,1)S(1)} %collective-permute-done.7.message, bf16[1280,256]{1,0:T(8,128)(2,1)S(1)} %shard_map.120.ext, bf16[256,256]{1,0:T(8,128)(2,1)S(1)} %copy-done.3, ...), custom_call_target="tpu_custom_call", output_to_operand_aliasing={{1}: (3, {}), {2}: (4, {})} | custom-call | flops 1000000000 | bytes 4000000 | tf_op jit(solution)/shard_map/slot/pallas_call | solution.py:279
  65.3 5.3 %collective-permute-done.10.message = bf16[1088,256]{1,0:T(8,128)(2,1)S(1)} collective-permute-done((bf16[1088,256]{1,0:T(8,128)(2,1)S(1)}, bf16[1088,256]{1,0:T(8,128)(2,1)S(1)}, u32[]{:S(2)}, u32[]{:S(2)}) %collective-permute-start.10) | collective-permute-done | bytes 557088 | tf_op jit(solution)/shard_map/ppermute | solution.py:311
  70.6 3.0 %slot.9 = (f32[8,1024]{1,0:T(8,128)S(1)}, f32[1280,256]{1,0:T(8,128)S(1)}, f32[256,256]{1,0:T(8,128)S(1)}) custom-call(bf16[1088,256]{1,0:T(8,128)(2,1)S(1)} %collective-permute-done.10.message, bf16[1280,256]{1,0:T(8,128)(2,1)S(1)} %shard_map.120.ext, bf16[256,256]{1,0:T(8,128)(2,1)S(1)} %copy-done.3, ...), custom_call_target="tpu_custom_call", output_to_operand_aliasing={{1}: (3, {}), {2}: (4, {})} | custom-call | flops 1000000000 | bytes 4000000 | tf_op jit(solution)/shard_map/slot/pallas_call | solution.py:279
  74.1 1.9 %collective-permute-start.13 = (f32[256,256]{1,0:T(8,128)S(1)}, f32[256,256]{1,0:T(8,128)S(1)}, u32[]{:S(2)}, u32[]{:S(2)}) collective-permute-start(f32[256,256]{1,0:T(8,128)S(1)} %get-tuple-element.59), channel_id=1, source_target_pairs={{0,8},{8,0},{1,9},{9,1},{2,10},{10,2},{3,11},{11,3},{4,12},{12,4},... | collective-permute-start | bytes 786440 | tf_op jit(solution)/shard_map/ppermute | solution.py:347
  76.0 14.1 %collective-permute-start.6 = (f32[8,1024]{1,0:T(8,128)S(1)}, f32[8,1024]{1,0:T(8,128)S(1)}, u32[]{:S(2)}, u32[]{:S(2)}) collective-permute-start(f32[8,1024]{1,0:T(8,128)S(1)} %get-tuple-element.45), channel_id=1, source_target_pairs={{0,16},{8,24},{16,32},{24,40},{32,48},{40,56},{48,64},{56,72},{64,... | collective-permute-start | bytes 98312 | tf_op jit(solution)/shard_map/ppermute | solution.py:311
  90.1 6.9 %collective-permute-start.11 = (f32[8,1024]{1,0:T(8,128)S(1)}, f32[8,1024]{1,0:T(8,128)S(1)}, u32[]{:S(2)}, u32[]{:S(2)}) collective-permute-start(f32[8,1024]{1,0:T(8,128)S(1)} %get-tuple-element.54), channel_id=1, source_target_pairs={{0,64},{8,72},{16,80},{24,88},{32,96},{40,104},{48,112},{56,120},{... | collective-permute-start | bytes 98312 | tf_op jit(solution)/shard_map/ppermute | solution.py:311
  97.0 4.5 %collective-permute-start.9 = (f32[8,1024]{1,0:T(8,128)S(1)}, f32[8,1024]{1,0:T(8,128)S(1)}, u32[]{:S(2)}, u32[]{:S(2)}) collective-permute-start(f32[8,1024]{1,0:T(8,128)S(1)} %get-tuple-element.51), channel_id=1, source_target_pairs={{0,32},{8,40},{16,48},{24,56},{32,64},{40,72},{48,80},{56,88},{64,... | collective-permute-start | bytes 98312 | tf_op jit(solution)/shard_map/ppermute | solution.py:311
  101.5 5.7 %collective-permute-start.12 = (f32[8,1024]{1,0:T(8,128)S(1)}, f32[8,1024]{1,0:T(8,128)S(1)}, u32[]{:S(2)}, u32[]{:S(2)}) collective-permute-start(f32[8,1024]{1,0:T(8,128)S(1)} %get-tuple-element.55), channel_id=1, source_target_pairs={{0,128},{8,136},{16,144},{24,152},{32,160},{40,168},{48,176},{56,1... | collective-permute-start | bytes 98312 | tf_op jit(solution)/shard_map/ppermute | solution.py:311
  107.3 1.5 collective-permute-start.5
  110.4 29.2 %all_to_all.18 = f32[256,1,384]{2,1,0:T(1,128)S(1)} all-to-all(f32[256,1,384]{2,1,0:T(1,128)S(1)} %copy.24), channel_id=1, replica_groups=mesh['pair'=32,'core'=2,'band'=8] {'pair','band'}, dimensions={0} | all-to-all | bytes 786432 | tf_op jit(solution)/shard_map/all_to_all | solution.py:356
  140.0 23.6 %all_to_all.19 = f32[256,1,384]{2,1,0:T(1,128)S(1)} all-to-all(f32[256,1,384]{2,1,0:T(1,128)S(1)} %reshape.38), channel_id=1, replica_groups=mesh['pair'=32,'core'=2,'band'=8] {'pair','band'}, dimensions={0} | all-to-all | bytes 786432 | tf_op jit(solution)/shard_map/all_to_all | solution.py:361
  163.7 1.9 %collective-permute-start.16 = (f32[256,384]{1,0:T(8,128)S(1)}, f32[256,384]{1,0:T(8,128)S(1)}, u32[]{:S(2)}, u32[]{:S(2)}) collective-permute-start(f32[256,384]{1,0:T(8,128)S(1)} %bitcast.21), channel_id=1, source_target_pairs={{0,8},{8,0},{1,9},{9,1},{2,10},{10,2},{3,11},{11,3},{4,12},{12,4},... | collective-permute-start | bytes 1179656 | tf_op jit(solution)/shard_map/ppermute | solution.py:366
  165.6 6.6 %collective-permute-start.14 = (bf16[128,256]{1,0:T(8,128)(2,1)S(1)}, bf16[128,256]{1,0:T(8,128)(2,1)S(1)}, u32[]{:S(2)}, u32[]{:S(2)}) collective-permute-start(bf16[128,256]{1,0:T(8,128)(2,1)S(1)} %get-tuple-element.61), channel_id=1, source_target_pairs={{0,1},{1,2},{2,3},{3,4},{4,5},{5,6},{6,7},{8,9},{9,10},{10,11},{11... | collective-permute-start | bytes 196616 | tf_op jit(solution)/shard_map/ppermute | solution.py:311
  172.3 1.9 %collective-permute-start.15 = (bf16[128,256]{1,0:T(8,128)(2,1)S(1)}, bf16[128,256]{1,0:T(8,128)(2,1)S(1)}, u32[]{:S(2)}, u32[]{:S(2)}) collective-permute-start(bf16[128,256]{1,0:T(8,128)(2,1)S(1)} %get-tuple-element.62), channel_id=1, source_target_pairs={{1,0},{2,1},{3,2},{4,3},{5,4},{6,5},{7,6},{9,8},{10,9},{11,10},{12... | collective-permute-start | bytes 196616 | tf_op jit(solution)/shard_map/ppermute | solution.py:311
  174.3 10.2 %collective-permute-done.15.from_next = bf16[128,256]{1,0:T(8,128)(2,1)S(1)} collective-permute-done((bf16[128,256]{1,0:T(8,128)(2,1)S(1)}, bf16[128,256]{1,0:T(8,128)(2,1)S(1)}, u32[]{:S(2)}, u32[]{:S(2)}) %collective-permute-start.15) | collective-permute-done | bytes 65568 | tf_op jit(solution)/shard_map/ppermute | solution.py:311
  184.5 1.4 shard_map.123
  186.0 0.7 copy.25
  186.7 0.8 slice_select_fusion
  (37 shorter events, 4.3 us)
Async XLA Ops:
  0.6 0.7 copy-start.4
  6.7 19.2 %copy-start = (bf16[1,8,128,256]{3,2,1,0:T(8,128)(2,1)S(1)}, bf16[1,8,128,256]{3,2,1,0:T(8,128)(2,1)}, u32[]{:S(2)}) copy-start(bf16[1,8,128,256]{3,2,1,0:T(8,128)(2,1)} %param.9) | copy-start | bytes 1572868
  6.7 17.8 %collective-permute-start.1 = (bf16[1216,256]{1,0:T(8,128)(2,1)S(1)}, bf16[1216,256]{1,0:T(8,128)(2,1)S(1)}, u32[]{:S(2)}, u32[]{:S(2)}) collective-permute-start(bf16[1216,256]{1,0:T(8,128)(2,1)S(1)} %get-tuple-element.38), channel_id=1, source_target_pairs={{16,0},{24,8},{32,16},{40,24},{48,32},{56,40},{64,48},{72,56},{80,... | collective-permute-start | bytes 1867784 | tf_op jit(solution)/shard_map/ppermute | solution.py:311
  8.1 47.9 %collective-permute-start = (bf16[1088,256]{1,0:T(8,128)(2,1)S(1)}, bf16[1088,256]{1,0:T(8,128)(2,1)S(1)}, u32[]{:S(2)}, u32[]{:S(2)}) collective-permute-start(bf16[1088,256]{1,0:T(8,128)(2,1)S(1)} %get-tuple-element.37), channel_id=1, source_target_pairs={{8,0},{24,16},{40,32},{56,48},{72,64},{88,80},{104,96},{120,112},{... | collective-permute-start | bytes 1671176 | tf_op jit(solution)/shard_map/ppermute | solution.py:326
  9.4 43.4 %copy-start.2 = (bf16[256,256]{1,0:T(8,128)(2,1)S(1)}, bf16[256,256]{1,0:T(8,128)(2,1)}, u32[]{:S(2)}) copy-start(bf16[256,256]{1,0:T(8,128)(2,1)} %w_value.3) | copy-start | bytes 393220
  9.4 49.8 %collective-permute-start.8 = (bf16[1152,256]{1,0:T(8,128)(2,1)S(1)}, bf16[1152,256]{1,0:T(8,128)(2,1)S(1)}, u32[]{:S(2)}, u32[]{:S(2)}) collective-permute-start(bf16[1152,256]{1,0:T(8,128)(2,1)S(1)} %get-tuple-element.46), channel_id=1, source_target_pairs={{128,0},{136,8},{144,16},{152,24},{160,32},{168,40},{176,48},{184,... | collective-permute-start | bytes 1769480 | tf_op jit(solution)/shard_map/ppermute | solution.py:311
  24.6 31.5 %collective-permute-start.2 = (bf16[1088,256]{1,0:T(8,128)(2,1)S(1)}, bf16[1088,256]{1,0:T(8,128)(2,1)S(1)}, u32[]{:S(2)}, u32[]{:S(2)}) collective-permute-start(bf16[1088,256]{1,0:T(8,128)(2,1)S(1)} %get-tuple-element.75), channel_id=1, source_target_pairs={{0,8},{16,24},{32,40},{48,56},{64,72},{80,88},{96,104},{112,120},{... | collective-permute-start | bytes 1671176 | tf_op jit(solution)/shard_map/ppermute | solution.py:329
  25.9 27.1 %copy-start.3 = (bf16[256,256]{1,0:T(8,128)(2,1)S(1)}, bf16[256,256]{1,0:T(8,128)(2,1)}, u32[]{:S(2)}) copy-start(bf16[256,256]{1,0:T(8,128)(2,1)} %w_out.9) | copy-start | bytes 393220
  25.9 12.9 %collective-permute-start.3 = (bf16[128,256]{1,0:T(8,128)(2,1)S(1)}, bf16[128,256]{1,0:T(8,128)(2,1)S(1)}, u32[]{:S(2)}, u32[]{:S(2)}) collective-permute-start(bf16[128,256]{1,0:T(8,128)(2,1)S(1)} %get-tuple-element.77), channel_id=1, source_target_pairs={{0,1},{1,2},{2,3},{3,4},{4,5},{5,6},{6,7},{8,9},{9,10},{10,11},{11... | collective-permute-start | bytes 196616 | tf_op jit(solution)/shard_map/ppermute | solution.py:311
  36.9 25.4 %collective-permute-start.7 = (bf16[1088,256]{1,0:T(8,128)(2,1)S(1)}, bf16[1088,256]{1,0:T(8,128)(2,1)S(1)}, u32[]{:S(2)}, u32[]{:S(2)}) collective-permute-start(bf16[1088,256]{1,0:T(8,128)(2,1)S(1)} %get-tuple-element.74), channel_id=1, source_target_pairs={{16,0},{24,8},{32,16},{40,24},{48,32},{56,40},{64,48},{72,56},{80,... | collective-permute-start | bytes 1671176 | tf_op jit(solution)/shard_map/ppermute | solution.py:311
  38.8 12.5 %collective-permute-start.4 = (bf16[128,256]{1,0:T(8,128)(2,1)S(1)}, bf16[128,256]{1,0:T(8,128)(2,1)S(1)}, u32[]{:S(2)}, u32[]{:S(2)}) collective-permute-start(bf16[128,256]{1,0:T(8,128)(2,1)S(1)} %get-tuple-element.76), channel_id=1, source_target_pairs={{1,0},{2,1},{3,2},{4,3},{5,4},{6,5},{7,6},{9,8},{10,9},{11,10},{12... | collective-permute-start | bytes 196616 | tf_op jit(solution)/shard_map/ppermute | solution.py:311
  51.3 19.3 %collective-permute-start.10 = (bf16[1088,256]{1,0:T(8,128)(2,1)S(1)}, bf16[1088,256]{1,0:T(8,128)(2,1)S(1)}, u32[]{:S(2)}, u32[]{:S(2)}) collective-permute-start(bf16[1088,256]{1,0:T(8,128)(2,1)S(1)} %slice.42), channel_id=1, source_target_pairs={{64,0},{72,8},{80,16},{88,24},{96,32},{104,40},{112,48},{120,56},{... | collective-permute-start | bytes 1671176 | tf_op jit(solution)/shard_map/ppermute | solution.py:311
  74.1 35.4 %collective-permute-start.13 = (f32[256,256]{1,0:T(8,128)S(1)}, f32[256,256]{1,0:T(8,128)S(1)}, u32[]{:S(2)}, u32[]{:S(2)}) collective-permute-start(f32[256,256]{1,0:T(8,128)S(1)} %get-tuple-element.59), channel_id=1, source_target_pairs={{0,8},{8,0},{1,9},{9,1},{2,10},{10,2},{3,11},{11,3},{4,12},{12,4},... | collective-permute-start | bytes 786440 | tf_op jit(solution)/shard_map/ppermute | solution.py:347
  76.0 31.3 %collective-permute-start.6 = (f32[8,1024]{1,0:T(8,128)S(1)}, f32[8,1024]{1,0:T(8,128)S(1)}, u32[]{:S(2)}, u32[]{:S(2)}) collective-permute-start(f32[8,1024]{1,0:T(8,128)S(1)} %get-tuple-element.45), channel_id=1, source_target_pairs={{0,16},{8,24},{16,32},{24,40},{32,48},{40,56},{48,64},{56,72},{64,... | collective-permute-start | bytes 98312 | tf_op jit(solution)/shard_map/ppermute | solution.py:311
  90.1 18.7 %collective-permute-start.11 = (f32[8,1024]{1,0:T(8,128)S(1)}, f32[8,1024]{1,0:T(8,128)S(1)}, u32[]{:S(2)}, u32[]{:S(2)}) collective-permute-start(f32[8,1024]{1,0:T(8,128)S(1)} %get-tuple-element.54), channel_id=1, source_target_pairs={{0,64},{8,72},{16,80},{24,88},{32,96},{40,104},{48,112},{56,120},{... | collective-permute-start | bytes 98312 | tf_op jit(solution)/shard_map/ppermute | solution.py:311
  97.0 11.8 %collective-permute-start.9 = (f32[8,1024]{1,0:T(8,128)S(1)}, f32[8,1024]{1,0:T(8,128)S(1)}, u32[]{:S(2)}, u32[]{:S(2)}) collective-permute-start(f32[8,1024]{1,0:T(8,128)S(1)} %get-tuple-element.51), channel_id=1, source_target_pairs={{0,32},{8,40},{16,48},{24,56},{32,64},{40,72},{48,80},{56,88},{64,... | collective-permute-start | bytes 98312 | tf_op jit(solution)/shard_map/ppermute | solution.py:311
  101.5 7.3 %collective-permute-start.12 = (f32[8,1024]{1,0:T(8,128)S(1)}, f32[8,1024]{1,0:T(8,128)S(1)}, u32[]{:S(2)}, u32[]{:S(2)}) collective-permute-start(f32[8,1024]{1,0:T(8,128)S(1)} %get-tuple-element.55), channel_id=1, source_target_pairs={{0,128},{8,136},{16,144},{24,152},{32,160},{40,168},{48,176},{56,1... | collective-permute-start | bytes 98312 | tf_op jit(solution)/shard_map/ppermute | solution.py:311
  107.3 2.1 %collective-permute-start.5 = (f32[8,1024]{1,0:T(8,128)S(1)}, f32[8,1024]{1,0:T(8,128)S(1)}, u32[]{:S(2)}, u32[]{:S(2)}) collective-permute-start(f32[8,1024]{1,0:T(8,128)S(1)} %get-tuple-element.44), channel_id=1, source_target_pairs={{0,8},{8,16},{16,24},{24,32},{32,40},{40,48},{48,56},{56,64},{64,7... | collective-permute-start | bytes 98312 | tf_op jit(solution)/shard_map/ppermute | solution.py:311
  139.5 45.0 %copy-start.1 = (bf16[1,8,128,256]{3,2,1,0:T(8,128)(2,1)S(1)}, bf16[1,8,128,256]{3,2,1,0:T(8,128)(2,1)}, u32[]{:S(2)}) copy-start(bf16[1,8,128,256]{3,2,1,0:T(8,128)(2,1)} %param.10) | copy-start | bytes 1572868
  163.7 22.3 %collective-permute-start.16 = (f32[256,384]{1,0:T(8,128)S(1)}, f32[256,384]{1,0:T(8,128)S(1)}, u32[]{:S(2)}, u32[]{:S(2)}) collective-permute-start(f32[256,384]{1,0:T(8,128)S(1)} %bitcast.21), channel_id=1, source_target_pairs={{0,8},{8,0},{1,9},{9,1},{2,10},{10,2},{3,11},{11,3},{4,12},{12,4},... | collective-permute-start | bytes 1179656 | tf_op jit(solution)/shard_map/ppermute | solution.py:366
  165.6 8.6 %collective-permute-start.14 = (bf16[128,256]{1,0:T(8,128)(2,1)S(1)}, bf16[128,256]{1,0:T(8,128)(2,1)S(1)}, u32[]{:S(2)}, u32[]{:S(2)}) collective-permute-start(bf16[128,256]{1,0:T(8,128)(2,1)S(1)} %get-tuple-element.61), channel_id=1, source_target_pairs={{0,1},{1,2},{2,3},{3,4},{4,5},{5,6},{6,7},{8,9},{9,10},{10,11},{11... | collective-permute-start | bytes 196616 | tf_op jit(solution)/shard_map/ppermute | solution.py:311
  172.3 12.2 %collective-permute-start.15 = (bf16[128,256]{1,0:T(8,128)(2,1)S(1)}, bf16[128,256]{1,0:T(8,128)(2,1)S(1)}, u32[]{:S(2)}, u32[]{:S(2)}) collective-permute-start(bf16[128,256]{1,0:T(8,128)(2,1)S(1)} %get-tuple-element.62), channel_id=1, source_target_pairs={{1,0},{2,1},{3,2},{4,3},{5,4},{6,5},{7,6},{9,8},{10,9},{11,10},{12... | collective-permute-start | bytes 196616 | tf_op jit(solution)/shard_map/ppermute | solution.py:311
